TPU v7x, 32 devices: a whole 2x2x4 slice. The times are simulated.
32 devices in a mesh: wide: 16 (over z, y, core), narrow: 2 (over x).
Axes of the slice: x: 2, y: 2, z: 4, core: 2. Of those that a mesh axis runs over, the one named last changes fastest.
Arguments:
- tokens: bfloat16 [128, 8, 64, 768], P('wide', None, 'narrow'), may hold values from -6 to 6
- masked: int32 [128, 8, 64], P('wide', None, 'narrow'), may hold values 0 or 1
- resolution: int32 [128], P('wide'), may hold values from 0 to 1, as said below
- mask_embed: bfloat16 [768], replicated, may hold values from -5 to 5
- gains: bfloat16 [768, 2], replicated, may hold values from 0.5 to 1.5
- biases: bfloat16 [768, 6], replicated, may hold values from -1 to 1
- w_qkv: bfloat16 [768, 2304], replicated, may hold values from -0.21875 to 0.21875
- w_proj: bfloat16 [768, 768], replicated, may hold values from -1.75 to 1.75
- w_fc1: bfloat16 [768, 3072], replicated, may hold values from -0.21875 to 0.21875
- fc1_bias: bfloat16 [3072], replicated, may hold values from -1 to 1
- w_fc2: bfloat16 [3072, 768], replicated, may hold values from -0.109375 to 0.109375
- cotangent: bfloat16 [128, 8, 64, 768], P('wide', None, 'narrow'), may hold values from -6 to 6
Outputs:
- output: bfloat16 [128, 8, 64, 768], P('wide', None, 'narrow')
- grad_tokens: bfloat16 [128, 8, 64, 768], P('wide', None, 'narrow')
- grad_mask_embed: float32 [768], P(('wide', 'narrow'))
- grad_gains: float32 [768, 2], P(('wide', 'narrow'))
- grad_biases: float32 [768, 6], P(('wide', 'narrow'))
- grad_qkv: float32 [768, 2304], P(('wide', 'narrow'))
- grad_proj: float32 [768, 768], P(('wide', 'narrow'))
- grad_fc1: float32 [768, 3072], P(('wide', 'narrow'))
- grad_fc1_bias: float32 [3072], P(('wide', 'narrow'))
- grad_fc2: float32 [3072, 768], P(('wide', 'narrow'))
Inputs may be any that keep to these rules, and one draw needn't show every extreme that they name: `resolution`: 1 marks a clip of 128 mel bins, 0 a clip of 64 mel bins whose frequency rows 4 and above are empty; clips of 128 mel bins come first and both kinds occur.
All inputs are finite; a program needn't handle non-finite values. No bound on the sum of `masked` on one device may be relied on, other than what follows from the above.
Results may differ from a plain program's by a relative error of at most 0.013.
Values may be sent and summed in bfloat16 or wider, within the bound.
No kernel may reach another device: no remote copies, remote signals or barrier semaphores. Data moves between devices by JAX's collectives and lax.ppermute only.
A program may use at most 448 MiB of HBM per device.

v0:
```python
import jax
import jax.numpy as jnp
from jax import lax
from jax.sharding import PartitionSpec as P

HEADS = 12


epsilon = 1e-06


def norm_rows(matrix, gain_vec, shift_vec):
    row_mean = jnp.mean(matrix, axis=-1, keepdims=True)
    centred = matrix - row_mean
    spread = jnp.mean(centred * centred, axis=-1, keepdims=True)
    return centred * lax.rsqrt(spread + epsilon) * gain_vec + shift_vec


def gelu_exact(values):
    return jax.nn.gelu(values, approximate=False)


def slot_valid(resolution, freq_rows, columns):
    upper = (resolution[:, None] == 1) | (jnp.arange(freq_rows)[None, :] < freq_rows // 2)
    spread_out = jnp.broadcast_to(upper[:, :, None], (resolution.shape[0], freq_rows, columns))
    return spread_out.reshape(resolution.shape[0], freq_rows * columns)


def scores_of(head_queries, head_keys, key_valid, score_scale):
    raw_scores = (
        jnp.einsum("cqhe,ckhe->chqk", head_queries, head_keys, preferred_element_type=jnp.float32)
        * score_scale
    )
    return jnp.where(key_valid[:, None, None, :], raw_scores, -1e30)


def body(
    tokens,
    masked,
    resolution,
    mask_embed,
    gains,
    biases,
    w_qkv,
    w_proj,
    w_fc1,
    fc1_bias,
    w_fc2,
    cotangent,
):
    clip_count, freq_rows, local_cols, model_width = tokens.shape
    head_count = HEADS
    head_width = model_width // head_count
    score_scale = head_width ** (-0.5)
    row_count = clip_count * freq_rows * local_cols
    token_shape = (clip_count, freq_rows * local_cols, head_count, head_width)
    local_shape = (clip_count, freq_rows, local_cols, model_width)
    is_masked = (masked == 1).reshape(row_count, 1)
    query_valid = slot_valid(resolution, freq_rows, local_cols).reshape(row_count, 1)
    embedding = mask_embed.astype(jnp.float32)
    entered = jnp.where(
        is_masked, embedding[None, :], tokens.reshape(row_count, model_width).astype(jnp.float32)
    )
    float_gains = gains.astype(jnp.float32)
    float_biases = biases.astype(jnp.float32)
    normed_one, norm_one_back = jax.vjp(norm_rows, entered, float_gains[:, 0], float_biases[:, 4])
    low_one = normed_one.astype(jnp.bfloat16)
    projected = jnp.dot(low_one, w_qkv, preferred_element_type=jnp.float32)
    queries = (projected[:, :model_width] + float_biases[:, 0]).astype(jnp.bfloat16)
    key_rows = projected[:, model_width : 2 * model_width].astype(jnp.bfloat16).reshape(local_shape)
    value_rows = (
        (projected[:, 2 * model_width :] + float_biases[:, 1])
        .astype(jnp.bfloat16)
        .reshape(local_shape)
    )
    key_all, value_all = (
        lax.all_gather(key_rows, "narrow", axis=2, tiled=True),
        lax.all_gather(value_rows, "narrow", axis=2, tiled=True),
    )
    all_cols = key_all.shape[2]
    all_shape = (clip_count, freq_rows * all_cols, head_count, head_width)
    key_valid = slot_valid(resolution, freq_rows, all_cols)
    head_queries = queries.reshape(token_shape)
    scores = scores_of(head_queries, key_all.reshape(all_shape), key_valid, score_scale)
    top = jnp.max(scores, axis=-1, keepdims=True)
    shifted = jnp.exp(scores - top)
    total = jnp.sum(shifted, axis=-1, keepdims=True)
    log_total = top + jnp.log(total)
    probs = (shifted / total).astype(jnp.bfloat16)
    attended = jnp.einsum(
        "chqk,ckhe->cqhe", probs, value_all.reshape(all_shape), preferred_element_type=jnp.float32
    )
    attended = attended.astype(jnp.bfloat16).reshape(row_count, model_width)
    middle = (
        entered + jnp.dot(attended, w_proj, preferred_element_type=jnp.float32) + float_biases[:, 2]
    )
    normed_two, norm_two_back = jax.vjp(norm_rows, middle, float_gains[:, 1], float_biases[:, 5])
    low_two = normed_two.astype(jnp.bfloat16)
    hidden_pre = jnp.dot(low_two, w_fc1, preferred_element_type=jnp.float32) + fc1_bias.astype(
        jnp.float32
    )
    activated, gelu_back = jax.vjp(gelu_exact, hidden_pre)
    act_low = activated.astype(jnp.bfloat16)
    mlp_out = jnp.dot(act_low, w_fc2, preferred_element_type=jnp.float32) + float_biases[:, 3]
    output = (
        jnp.where(query_valid, middle + mlp_out, 0.0).astype(jnp.bfloat16).reshape(tokens.shape)
    )
    upstream = jnp.where(
        query_valid, cotangent.reshape(row_count, model_width).astype(jnp.float32), 0.0
    )
    up_low = upstream.astype(jnp.bfloat16)
    grad_fc2 = jnp.einsum("rf,rd->fd", act_low, up_low, preferred_element_type=jnp.float32)
    grad_out_bias = jnp.sum(up_low.astype(jnp.float32), axis=0)
    grad_act = jnp.einsum("rd,fd->rf", up_low, w_fc2, preferred_element_type=jnp.float32)
    grad_pre = gelu_back(grad_act)[0].astype(jnp.bfloat16)
    grad_fc1 = jnp.einsum("rd,rf->df", low_two, grad_pre, preferred_element_type=jnp.float32)
    grad_fc1_bias = jnp.sum(grad_pre.astype(jnp.float32), axis=0)
    grad_normed_two = jnp.einsum("rf,df->rd", grad_pre, w_fc1, preferred_element_type=jnp.float32)
    grad_middle_part, grad_gain_two, grad_shift_two = norm_two_back(grad_normed_two)
    grad_middle = upstream + grad_middle_part
    middle_low = grad_middle.astype(jnp.bfloat16)
    grad_proj = jnp.einsum("rd,re->de", attended, middle_low, preferred_element_type=jnp.float32)
    grad_proj_bias = jnp.sum(middle_low.astype(jnp.float32), axis=0)
    grad_attended = jnp.einsum("re,de->rd", middle_low, w_proj, preferred_element_type=jnp.float32)
    grad_attended = grad_attended.astype(jnp.bfloat16).reshape(token_shape)
    key_again, value_again = (
        lax.all_gather(key_rows, "narrow", axis=2, tiled=True),
        lax.all_gather(value_rows, "narrow", axis=2, tiled=True),
    )
    head_keys = key_again.reshape(all_shape)
    head_values = value_again.reshape(all_shape)
    probs_full = jnp.exp(scores_of(head_queries, head_keys, key_valid, score_scale) - log_total)
    grad_probs = jnp.einsum(
        "cqhe,ckhe->chqk", grad_attended, head_values, preferred_element_type=jnp.float32
    )
    inner = jnp.sum(probs_full * grad_probs, axis=-1, keepdims=True)
    grad_scores = (probs_full * (grad_probs - inner)).astype(jnp.bfloat16)
    grad_queries = (
        jnp.einsum("chqk,ckhe->cqhe", grad_scores, head_keys, preferred_element_type=jnp.float32)
        * score_scale
    )
    grad_queries = grad_queries.astype(jnp.bfloat16).reshape(row_count, model_width)
    probs_low = probs_full.astype(jnp.bfloat16)
    value_part = jnp.einsum(
        "chqk,cqhe->ckhe", probs_low, grad_attended, preferred_element_type=jnp.float32
    )
    key_part = (
        jnp.einsum("chqk,cqhe->ckhe", grad_scores, head_queries, preferred_element_type=jnp.float32)
        * score_scale
    )
    full_shape = (clip_count, freq_rows, all_cols, model_width)
    key_sum, value_sum = (
        lax.psum_scatter(
            key_part.reshape(full_shape).astype(jnp.bfloat16),
            "narrow",
            scatter_dimension=2,
            tiled=True,
        ).astype(jnp.float32),
        lax.psum_scatter(
            value_part.reshape(full_shape).astype(jnp.bfloat16),
            "narrow",
            scatter_dimension=2,
            tiled=True,
        ).astype(jnp.float32),
    )
    grad_keys = key_sum.astype(jnp.bfloat16).reshape(row_count, model_width)
    grad_values = value_sum.astype(jnp.bfloat16).reshape(row_count, model_width)
    grad_projected = jnp.concatenate([grad_queries, grad_keys, grad_values], axis=1)
    grad_qkv = jnp.einsum("rd,re->de", low_one, grad_projected, preferred_element_type=jnp.float32)
    grad_query_bias = jnp.sum(grad_queries.astype(jnp.float32), axis=0)
    grad_value_bias = jnp.sum(grad_values.astype(jnp.float32), axis=0)
    grad_normed_one = jnp.einsum(
        "re,de->rd", grad_projected, w_qkv, preferred_element_type=jnp.float32
    )
    grad_entered_part, grad_gain_one, grad_shift_one = norm_one_back(grad_normed_one)
    grad_entered = grad_middle + grad_entered_part
    grad_tokens = jnp.where(is_masked, 0.0, grad_entered).astype(jnp.bfloat16).reshape(tokens.shape)
    grad_embed = jnp.sum(jnp.where(is_masked, grad_entered, 0.0), axis=0)
    grad_gains = jnp.stack([grad_gain_one, grad_gain_two], axis=1)
    grad_biases = jnp.stack(
        [
            grad_query_bias,
            grad_value_bias,
            grad_proj_bias,
            grad_out_bias,
            grad_shift_one,
            grad_shift_two,
        ],
        axis=1,
    )
    summed = (
        lax.psum_scatter(grad_embed, ("wide", "narrow"), scatter_dimension=0, tiled=True),
        lax.psum_scatter(grad_gains, ("wide", "narrow"), scatter_dimension=0, tiled=True),
        lax.psum_scatter(grad_biases, ("wide", "narrow"), scatter_dimension=0, tiled=True),
        lax.psum_scatter(grad_qkv, ("wide", "narrow"), scatter_dimension=0, tiled=True),
        lax.psum_scatter(grad_proj, ("wide", "narrow"), scatter_dimension=0, tiled=True),
        lax.psum_scatter(grad_fc1, ("wide", "narrow"), scatter_dimension=0, tiled=True),
        lax.psum_scatter(grad_fc1_bias, ("wide", "narrow"), scatter_dimension=0, tiled=True),
        lax.psum_scatter(grad_fc2, ("wide", "narrow"), scatter_dimension=0, tiled=True),
    )
    return (
        output,
        grad_tokens,
        summed[0],
        summed[1],
        summed[2],
        summed[3],
        summed[4],
        summed[5],
        summed[6],
        summed[7],
    )


def solution(mesh):
    return jax.shard_map(
        body,
        mesh=mesh,
        in_specs=(
            P("wide", None, "narrow", None),
            P("wide", None, "narrow"),
            P("wide"),
            P(),
            P(),
            P(),
            P(),
            P(),
            P(),
            P(),
            P(),
            P("wide", None, "narrow", None),
        ),
        out_specs=(
            P("wide", None, "narrow", None),
            P("wide", None, "narrow", None),
            P(("wide", "narrow")),
            P(("wide", "narrow"), None),
            P(("wide", "narrow"), None),
            P(("wide", "narrow"), None),
            P(("wide", "narrow"), None),
            P(("wide", "narrow"), None),
            P(("wide", "narrow")),
            P(("wide", "narrow"), None),
        ),
        check_vma=False,
    )
```

profile of v0, /device:TPU:0, one launch (start us, length us, event | category | flops | bytes accessed | tf_op | source)
XLA Modules:
  0.0 1247.9 jit_solution(10463331880875422992)
XLA Ops:
  65.1 62.2 %all-gather.3.cloned.1.call-done = bf16[8,8,64,768]{3,1,0,2:T(8,128)(2,1)} async-done(((bf16[8,8,32,768]{3,1,0,2:T(8,128)(2,1)}), bf16[8,8,64,768]{3,1,0,2:T(8,128)(2,1)}) %all-gather.3.cloned.1.call-update) | async-done | bytes 6291472 | tf_op jit(solution)/shard_map/all_gather | solution.py:78
  127.3 16.8 %copy.43 = bf16[8,8,64,768]{2,1,3,0:T(8,128)(2,1)} copy(bf16[8,8,64,768]{3,1,0,2:T(8,128)(2,1)} %all-gather.3.cloned.1.call-done) | data formatting | bytes 12582912 | tf_op jit(solution)/shard_map/all_gather | solution.py:78
  144.1 17.2 %reshape.236 = bf16[8,512,12,64]{1,3,2,0:T(8,128)(2,1)} reshape(bf16[8,8,64,768]{2,1,3,0:T(8,128)(2,1)} %copy.43) | data formatting | bytes 12582912 | tf_op jit(solution)/shard_map/reshape | solution.py:91
  161.3 47.9 %all-gather.5.cloned.1.call-done = bf16[8,8,64,768]{3,1,0,2:T(8,128)(2,1)} async-done(((bf16[8,8,32,768]{3,1,0,2:T(8,128)(2,1)}), bf16[8,8,64,768]{3,1,0,2:T(8,128)(2,1)}) %all-gather.5.cloned.1.call-update) | async-done | bytes 6291472 | tf_op jit(solution)/shard_map/all_gather | solution.py:77
  209.2 16.7 %copy.46 = bf16[8,8,64,768]{2,1,3,0:T(8,128)(2,1)} copy(bf16[8,8,64,768]{3,1,0,2:T(8,128)(2,1)} %all-gather.5.cloned.1.call-done) | data formatting | bytes 12582912 | tf_op jit(solution)/shard_map/all_gather | solution.py:77
  225.9 17.2 %reshape.239 = bf16[8,512,12,64]{1,3,2,0:T(8,128)(2,1)} reshape(bf16[8,8,64,768]{2,1,3,0:T(8,128)(2,1)} %copy.46) | data formatting | bytes 12582912 | tf_op jit(solution)/shard_map/reshape | solution.py:84
  243.1 22.0 %fusion.12 = (f32[8,12,256]{2,1,0:T(8,128)S(1)}, f32[8,12,256,512]{3,2,1,0:T(8,128)}) fusion(pred[8,512]{1,0:T(8,128)(4,1)S(1)} %broadcast_in_dim.120, bf16[8,512,12,64]{1,3,2,0:T(8,128)(2,1)} %reshape.239, bf16[8,256,12,64]{1,0,3,2:T(8,128)(2,1)} %bitcast.112), kind=kOutput, calls=%fused_computation.29 | convolution fusion | flops 1648336896 | bytes 59871232 | tf_op jit(solution)/shard_map/cqhe,ckhe->chqk/dot_general | solution.py:31
  265.1 21.7 %fusion = f32[8,12,256]{2,1,0:T(8,128)S(1)} fusion(f32[8,12,256]{2,1,0:T(8,128)S(1)} %get-tuple-element.40, f32[8,12,256,512]{3,2,1,0:T(8,128)} %get-tuple-element.41, pred[8,512]{1,0:T(8,128)(4,1)S(1)} %broadcast_in_dim.120), kind=kLoop, calls=%fused_computation.6 | loop fusion | flops 50307072 | bytes 50532352 | tf_op jit(solution)/shard_map/reduce_sum | solution.py:87
  287.4 21.3 %convert_bitcast_fusion.1 = bf16[8,256,12,64]{1,3,2,0:T(8,128)(2,1)S(1)} fusion(bf16[8,512,12,64]{1,3,2,0:T(8,128)(2,1)} %reshape.236, f32[8,12,256]{2,1,0:T(8,128)S(1)} %fusion, f32[8,12,256]{2,1,0:T(8,128)S(1)} %get-tuple-element.40, f32[8,12,256,512]{3,2,1,0:T(8,128)} %get-tuple-element.41, pred[8,512]{1,0:T(8,128)(4,1)S(1)} %broadcast_in_dim.120), kind=kOutput, calls=%fused_computation.73 | convolution fusion | flops 1675100160 | bytes 59969536 | tf_op jit(solution)/shard_map/chqk,ckhe->cqhe/dot_general | solution.py:90
  317.1 69.3 %multiply_convert_fusion.1 = (bf16[2048,3072]{1,0:T(8,128)(2,1)}, f32[2048,3072]{1,0:T(8,128)}, f32[2048,3072]{1,0:T(8,128)}) fusion(f32[3072]{0:T(1024)S(1)} %copy-done.46, bf16[768,3072]{1,0:T(8,128)(2,1)S(1)} %bitcast.130, f32[2048,768]{1,0:T(8,128)S(1)} %get-tuple-element.43, f32[768]{0:T(1024)S(1)} %copy-done.47, f32[768]{0:T(1024)S(1)} %copy-done.44, ...), kind=kOutput, calls=%fused_computation.14 | convolution fusion | flops 10086776832 | bytes 73959424 | tf_op jit(solution)/shard_map/dot_general | solution.py:99
  386.4 33.8 %convert_reduce_fusion = (f32[3072]{0:T(1024)}, bf16[2048,3072]{1,0:T(8,128)(2,1)}) fusion(f32[2048,3072]{1,0:T(8,128)} %get-tuple-element.37, bf16[2048,768]{1,0:T(8,128)(2,1)} %fusion.19, bf16[3072,768]{1,0:T(8,128)(2,1)} %param.22, f32[2048,3072]{1,0:T(8,128)} %get-tuple-element.44, f32[3072]{0:T(1024)} %convert_element_type.142), kind=kOutput, calls=%fused_computation.11 | convolution fusion | flops 9770628096 | bytes 70803456 | tf_op jit(solution)/shard_map/rd,fd->rf/dot_general | solution.py:114
  420.3 19.8 %multiply_reduce_fusion.1 = (f32[768]{0:T(1024)}, f32[2048]{0:T(1024)S(1)}, f32[768]{0:T(1024)}, f32[2048,768]{1,0:T(8,128)}) fusion(f32[2048,768]{1,0:T(8,128)} %copy-done.7, f32[2048]{0:T(1024)S(1)} %fusion.32, f32[2048]{0:T(1024)S(1)} %broadcast_multiply_fusion.1, f32[768]{0:T(1024)} %get-tuple-element.54, bf16[2048,3072]{1,0:T(8,128)(2,1)} %get-tuple-element.52, ...), kind=kOutput, calls=%fused_computation.47 | convolution fusion | flops 9676255232 | bytes 29918208 | tf_op jit(solution)/shard_map/rf,df->rd/dot_general | solution.py:118
  462.1 22.9 %convert_bitcast_fusion = bf16[8,512,12,64]{1,3,2,0:T(8,128)(2,1)} fusion(f32[8,12,256]{2,1,0:T(8,128)} %log_add_fusion, f32[8,12,256,512]{3,2,1,0:T(8,128)} %get-tuple-element.41, pred[8,512]{1,0:T(8,128)(4,1)S(1)} %copy-done.16, bf16[8,256,12,64]{1,0,3,2:T(8,128)(2,1)} %bitcast.114), kind=kOutput, calls=%fused_computation.53 | convolution fusion | flops 1664090112 | bytes 59871232 | tf_op jit(solution)/shard_map/chqk,cqhe->ckhe/dot_general | solution.py:144
  484.9 16.6 %convert_element_type.160 = bf16[8,8,64,768]{2,1,3,0:T(8,128)(2,1)} reshape(bf16[8,512,12,64]{1,3,2,0:T(8,128)(2,1)} %convert_bitcast_fusion) | data formatting | bytes 12582912 | tf_op jit(solution)/shard_map/convert_element_type | solution.py:160
  501.5 17.5 %copy.56 = bf16[8,8,64,768]{3,1,0,2:T(8,128)(2,1)} copy(bf16[8,8,64,768]{2,1,3,0:T(8,128)(2,1)} %convert_element_type.160) | data formatting | bytes 12582912 | tf_op jit(solution)/shard_map/convert_element_type | solution.py:160
  519.1 40.8 %multiply_reduce_fusion = (f32[8,12,256]{2,1,0:T(8,128)}, f32[8,12,256,512]{3,2,1,0:T(8,128)}) fusion(f32[8,12,256]{2,1,0:T(8,128)} %log_add_fusion, f32[8,12,256,512]{3,2,1,0:T(8,128)} %get-tuple-element.41, pred[8,512]{1,0:T(8,128)(4,1)S(1)} %copy-done.16, bf16[8,512,12,64]{1,3,2,0:T(8,128)(2,1)} %reshape.236, bf16[8,256,12,64]{1,0,3,2:T(8,128)(2,1)} %bitcast.115), kind=kOutput, calls=%fused_computation.1 | convolution fusion | flops 1673502720 | bytes 110301184 | tf_op jit(solution)/shard_map/cqhe,ckhe->chqk/dot_general | solution.py:133
  559.8 41.6 %multiply_convert_fusion = bf16[8,12,256,512]{3,2,1,0:T(8,128)(2,1)} fusion(f32[8,12,256,512]{3,2,1,0:T(8,128)} %get-tuple-element.47, f32[8,12,256]{2,1,0:T(8,128)} %get-tuple-element.46, f32[8,12,256]{2,1,0:T(8,128)} %log_add_fusion, f32[8,12,256,512]{3,2,1,0:T(8,128)} %get-tuple-element.41, pred[8,512]{1,0:T(8,128)(4,1)S(1)} %copy-done.16), kind=kLoop, calls=%fused_computation | loop fusion | flops 75497472 | bytes 126029824 | tf_op jit(solution)/shard_map/convert_element_type | solution.py:137
  633.2 17.5 %copy.53 = bf16[8,8,64,768]{3,1,0,2:T(8,128)(2,1)} copy(bf16[8,8,64,768]{2,1,3,0:T(8,128)(2,1)} %convert_element_type.156) | data formatting | bytes 12582912 | tf_op jit(solution)/shard_map/convert_element_type | solution.py:154
  674.7 18.6 %fusion.39 = f32[768,3072]{1,0:T(8,128)} fusion(bf16[2048,3072]{1,0:T(8,128)(2,1)} %get-tuple-element.52, f32[2048,768]{1,0:T(8,128)} %copy-done.7, f32[768]{0:T(1024)} %get-tuple-element.17, f32[768]{0:T(1024)} %get-tuple-element.54, f32[2048]{0:T(1024)S(1)} %copy-done.36, f32[2048]{0:T(1024)S(1)} %copy-done.26), kind=kOutput, calls=%fused_computation.111 | convolution fusion | flops 9671540736 | bytes 28334080 | tf_op jit(solution)/shard_map/rd,rf->df/dot_general | solution.py:116
  761.4 17.8 %select_convert_fusion.2 = bf16[2048,768]{1,0:T(8,128)(2,1)} fusion(f32[2048,768]{1,0:T(8,128)} %copy-done.7, bf16[2048,3072]{1,0:T(8,128)(2,1)} %get-tuple-element.36, bf16[3072,768]{1,0:T(8,128)(2,1)} %param.22, f32[768]{0:T(1024)} %get-tuple-element.16, pred[2048]{0:T(1024)(128)(4,1)} %copy-done.37), kind=kOutput, calls=%fused_computation.57 | convolution fusion | flops 9669967872 | bytes 26743808 | tf_op jit(solution)/shard_map/dot_general | solution.py:104
  811.6 40.9 %all-reduce.4 = (f32[768]{0:T(1024)}, f32[768,2]{0,1:T(2,128)}, f32[768,6]{0,1:T(8,128)}, f32[3072]{0:T(1024)}) all-reduce(f32[768]{0:T(1024)S(1)} %get-tuple-element.30, f32[768,2]{0,1:T(2,128)S(1)} %copy-done.40, f32[768,6]{0,1:T(8,128)} %stack.39, ...), channel_id=4, replica_groups=mesh['wide'=16,'narrow'=2] {'wide','narrow'}, use_global_device_ids=true, to_apply=%region_14.15.clone | all-reduce | flops 9984 | bytes 79872
  861.2 113.2 %reduce-scatter.19.cloned.1.call-done = f32[96,768]{1,0:T(8,128)} async-done(((f32[3072,768]{1,0:T(8,128)}), f32[96,768]{1,0:T(8,128)}) %reduce-scatter.19.cloned.1.call-update) | async-done | bytes 294928 | tf_op jit(solution)/shard_map/reduce_scatter | solution.py:199
  974.4 141.1 %reduce-scatter.17.cloned.1.call-done = f32[24,3072]{1,0:T(8,128)} async-done(((f32[768,3072]{1,0:T(8,128)}), f32[24,3072]{1,0:T(8,128)}) %reduce-scatter.17.cloned.1.call-update) | async-done | bytes 294928 | tf_op jit(solution)/shard_map/reduce_scatter | solution.py:197
  1115.5 125.3 %reduce-scatter.13.cloned.1.call-done = f32[24,2304]{1,0:T(8,128)} async-done(((f32[768,2304]{1,0:T(8,128)}), f32[24,2304]{1,0:T(8,128)}) %reduce-scatter.13.cloned.1.call-update) | async-done | bytes 221200 | tf_op jit(solution)/shard_map/reduce_scatter | solution.py:195
  (205 shorter events, 253.2 us)
Async XLA Ops:
  7.2 18.3 %copy-start = (bf16[768,2304]{1,0:T(8,128)(2,1)S(1)}, bf16[768,2304]{1,0:T(8,128)(2,1)}, u32[]{:S(2)}) copy-start(bf16[768,2304]{1,0:T(8,128)(2,1)} %param.18) | copy-start | bytes 10616836
  7.2 120.1 %all-gather.3.cloned.1.call-start = ((), (), s32[]{:S(2)}) async-start(), calls=%async_computation.6 | async-start | bytes 9437184 | tf_op jit(solution)/shard_map/all_gather | solution.py:78
  44.0 165.2 %all-gather.5.cloned.1.call-start = ((), (), s32[]{:S(2)}) async-start(), calls=%async_computation.7 | async-start | bytes 9437184 | tf_op jit(solution)/shard_map/all_gather | solution.py:77
  50.8 661.5 %reduce-scatter.11.cloned.1.call-start = ((), (), s32[]{:S(2)}) async-start(), calls=%async_computation.9 | async-start | bytes 9437184 | tf_op jit(solution)/shard_map/reduce_scatter | solution.py:159
  51.5 236.0 %copy-start.15 = (pred[8,512]{1,0:T(8,128)(4,1)}, pred[8,512]{1,0:T(8,128)(4,1)S(1)}, u32[]{:S(2)}) copy-start(pred[8,512]{1,0:T(8,128)(4,1)S(1)} %broadcast_in_dim.120) | copy-start | bytes 12292
  315.5 70.9 %copy-start.7 = (f32[2048,768]{1,0:T(8,128)}, f32[2048,768]{1,0:T(8,128)S(1)}, u32[]{:S(2)}) copy-start(f32[2048,768]{1,0:T(8,128)S(1)} %get-tuple-element.43) | copy-start | bytes 18874372
  315.6 124.5 %copy-start.25 = (f32[2048]{0:T(1024)}, f32[2048]{0:T(1024)S(1)}, u32[]{:S(2)}) copy-start(f32[2048]{0:T(1024)S(1)} %broadcast_multiply_fusion.1) | copy-start | bytes 24580
  317.1 123.1 %copy-start.35 = (f32[2048]{0:T(1024)}, f32[2048]{0:T(1024)S(1)}, u32[]{:S(2)}) copy-start(f32[2048]{0:T(1024)S(1)} %fusion.32) | copy-start | bytes 24580
  420.3 19.8 %copy-start.28 = (f32[2048]{0:T(1024)S(1)}, f32[2048]{0:T(1024)}, u32[]{:S(2)}) copy-start(f32[2048]{0:T(1024)} %copy-done.27) | copy-start | bytes 24580
  420.3 19.9 %copy-start.8 = (f32[2048,768]{1,0:T(8,128)S(1)}, f32[2048,768]{1,0:T(8,128)}, u32[]{:S(2)}) copy-start(f32[2048,768]{1,0:T(8,128)} %copy-done.7) | copy-start | bytes 18874372
  420.3 19.9 %copy-start.45 = (f32[768]{0:T(1024)S(1)}, f32[768]{0:T(1024)}, u32[]{:S(2)}) copy-start(f32[768]{0:T(1024)} %get-tuple-element.54) | copy-start | bytes 9220
  519.0 208.6 %reduce-scatter.9.cloned.1.call-start = ((), (), s32[]{:S(2)}) async-start(), calls=%async_computation.8 | async-start | bytes 9437184 | tf_op jit(solution)/shard_map/reduce_scatter | solution.py:153
  650.6 210.6 %reduce-scatter.15.cloned.1.call-start = ((), (), s32[]{:S(2)}) async-start(), calls=%async_computation.11 | async-start | bytes 2433024 | tf_op jit(solution)/shard_map/reduce_scatter | solution.py:196
  657.7 316.7 %reduce-scatter.19.cloned.1.call-start = ((), (), s32[]{:S(2)}) async-start(), calls=%async_computation.13 | async-start | bytes 9732096 | tf_op jit(solution)/shard_map/reduce_scatter | solution.py:199
  674.0 441.5 %reduce-scatter.17.cloned.1.call-start = ((), (), s32[]{:S(2)}) async-start(), calls=%async_computation.12 | async-start | bytes 9732096 | tf_op jit(solution)/shard_map/reduce_scatter | solution.py:197
  693.3 547.6 %reduce-scatter.13.cloned.1.call-start = ((), (), s32[]{:S(2)}) async-start(), calls=%async_computation.10 | async-start | bytes 7299072 | tf_op jit(solution)/shard_map/reduce_scatter | solution.py:195
  761.3 17.8 %copy-start.10 = (bf16[8,8,32,768]{3,1,0,2:T(8,128)(2,1)S(1)}, bf16[8,8,32,768]{3,1,0,2:T(8,128)(2,1)}, u32[]{:S(2)}) copy-start(bf16[8,8,32,768]{3,1,0,2:T(8,128)(2,1)} %reduce-scatter.11.cloned.1.call-done) | copy-start | bytes 9437188
  761.3 19.1 %copy-start.6 = (bf16[8,8,32,768]{3,2,1,0:T(8,128)(2,1)S(1)}, bf16[8,8,32,768]{3,2,1,0:T(8,128)(2,1)}, u32[]{:S(2)}) copy-start(bf16[8,8,32,768]{3,2,1,0:T(8,128)(2,1)} %param.12) | copy-start | bytes 9437188
  761.3 19.1 %copy-start.13 = (bf16[96,8,8,256]{3,1,2,0:T(8,128)(2,1)S(1)}, bf16[96,8,8,256]{3,1,2,0:T(8,128)(2,1)}, u32[]{:S(2)}) copy-start(bf16[96,8,8,256]{3,1,2,0:T(8,128)(2,1)} %copy.67) | copy-start | bytes 9437188
  761.3 19.1 %copy-start.19 = (f32[768]{0:T(1024)S(1)}, f32[768]{0:T(1024)}, u32[]{:S(2)}) copy-start(f32[768]{0:T(1024)} %copy-done.17) | copy-start | bytes 9220
  761.3 19.1 %copy-start.22 = (f32[2048]{0:T(1024)S(1)}, f32[2048]{0:T(1024)}, u32[]{:S(2)}) copy-start(f32[2048]{0:T(1024)} %div.47) | copy-start | bytes 24580
  761.3 19.1 %copy-start.24 = (f32[2048]{0:T(1024)S(1)}, f32[2048]{0:T(1024)}, u32[]{:S(2)}) copy-start(f32[2048]{0:T(1024)} %copy-done.23) | copy-start | bytes 24580
  761.4 19.1 %copy-start.32 = (pred[2048]{0:T(1024)(128)(4,1)S(1)}, pred[2048]{0:T(1024)(128)(4,1)}, u32[]{:S(2)}) copy-start(pred[2048]{0:T(1024)(128)(4,1)} %copy-done.30) | copy-start | bytes 6148
  761.4 19.1 %copy-start.34 = (f32[768]{0:T(1024)S(1)}, f32[768]{0:T(1024)}, u32[]{:S(2)}) copy-start(f32[768]{0:T(1024)} %copy-done.33) | copy-start | bytes 9220
  (38 other events, 203.1 us)
Sparse Core Ops, SparseCore 0:
  44.1 83.0 all-gather.2
  128.8 80.3 all-gather.4
  519.1 77.0 reduce-scatter.10
  650.8 76.8 reduce-scatter.8
  733.4 98.9 reduce-scatter.14
  839.7 134.6 reduce-scatter.18
  980.9 134.6 reduce-scatter.16
  1122.7 118.0 reduce-scatter.12
where the time goes:
time: 1260 us; the launch traced here: 1250 us
  waiting for transfers between devices  495 us (39%)
  matrix products  363 us (29%)
  local copies, waits for them, and re-layouts  219 us (17%)
  other arithmetic  114 us (9%)
  blocking collectives  40.9 us (3%)
  between operations  15 us (1%)
    reduce_scatter x1, waiting for transfers between devices, body(): lax.psum_scatter(grad_fc1, ('wide', 'narrow'), scatter_dimension=0, tiled...  141 us
    reduce_scatter x1, waiting for transfers between devices, body(): lax.psum_scatter(grad_qkv, ('wide', 'narrow'), scatter_dimension=0, tiled...  125 us
    reduce_scatter x1, waiting for transfers between devices, body(): lax.psum_scatter(grad_fc2, ('wide', 'narrow'), scatter_dimension=0, tiled...  113 us
    dot_general x1, matrix products, body(): jnp.dot(low_two, w_fc1, preferred_element_type=jnp.float32)  69.3 us
    all_gather x1, waiting for transfers between devices, body(): lax.all_gather(value_rows, 'narrow', axis=2, tiled=True)  62.2 us
    all_gather x1, waiting for transfers between devices, body(): lax.all_gather(key_rows, 'narrow', axis=2, tiled=True)  47.9 us
    convert_element_type x1, other arithmetic, body(): grad_scores = (probs_full * (grad_probs - inner)).astype(jnp.bfloat16)  41.6 us
    unnamed x1, blocking collectives  40.9 us
  transfers between devices with their start and end apart: 8, of which 6 were waited for; matrix products, arithmetic and copies ran while one was open for 28% of the time, Pallas kernels for 0%

commit v1 on v0

v1 whole, which is shorter than its diff:
```python
import functools

import jax
import jax.numpy as jnp
from jax import lax
from jax.experimental import pallas as pl
from jax.experimental.pallas import tpu as pltpu
from jax.sharding import PartitionSpec as P

HEADS = 12
EPS = 1e-06
LOG2E = 1.4426950408889634
F32 = jnp.float32
BF16 = jnp.bfloat16
MIB = 1 << 20


def dot_nn(a, b):
    return jnp.dot(a, b, preferred_element_type=F32)


def dot_nt(a, b):
    return lax.dot_general(a, b, (((1,), (1,)), ((), ())), preferred_element_type=F32)


def dot_tn(a, b):
    return lax.dot_general(a, b, (((0,), (0,)), ((), ())), preferred_element_type=F32)


def norm_stats(x):
    centred = x - jnp.mean(x, axis=-1, keepdims=True)
    rstd = lax.rsqrt(jnp.mean(centred * centred, axis=-1, keepdims=True) + EPS)
    return centred * rstd, rstd


def norm_back(grad, x, gain):
    xhat, rstd = norm_stats(x)
    scaled = grad * gain
    inner = jnp.mean(scaled * xhat, axis=-1, keepdims=True)
    outer = jnp.mean(scaled, axis=-1, keepdims=True)
    dx = rstd * (scaled - outer - xhat * inner)
    return dx, jnp.sum(grad * xhat, axis=0, keepdims=True), jnp.sum(grad, axis=0, keepdims=True)


def row_valid(rows, piece_rows, full):
    at = lax.broadcasted_iota(jnp.int32, (rows, 1), 0) % piece_rows
    return (at < piece_rows // 2) | full


def attn_fwd_kernel(c, pieces, info, *refs):
    xs = refs[:pieces]
    vec, wqkv, wproj = refs[pieces : pieces + 3]
    n1_o, qkv_o, att_o, lse_o, mid_o, n2_o = refs[-7:-1]
    lse_s = refs[-1]
    rp, d = xs[0].shape
    rows = rp * pieces
    hw = d // HEADS
    full = info[1 + c] == 1
    for i in range(pieces):
        xhat, _ = norm_stats(xs[i][...].astype(F32))
        n1_o[i * rp : (i + 1) * rp, :] = (xhat * vec[0:1, :] + vec[6:7, :]).astype(BF16)
    n1 = n1_o[...]
    qkv_o[:, 0:d] = (dot_nn(n1, wqkv[:, 0:d]) + vec[2:3, :]).astype(BF16)
    qkv_o[:, d : 2 * d] = dot_nn(n1, wqkv[:, d : 2 * d]).astype(BF16)
    qkv_o[:, 2 * d : 3 * d] = (dot_nn(n1, wqkv[:, 2 * d : 3 * d]) + vec[3:4, :]).astype(BF16)
    scale2 = hw**-0.5 * LOG2E
    bias = jnp.where(row_valid(rows, rp, full), 0.0, -1e30).astype(BF16)
    lane = lax.broadcasted_iota(jnp.int32, (1, 2 * hw), 1)
    head_lane = lax.broadcasted_iota(jnp.int32, (1, 128), 1)
    lse_s[...] = jnp.zeros_like(lse_s)

    def pair(p, carry):
        at = pl.multiple_of(p * 2 * hw, 2 * hw)
        q = qkv_o[:, pl.ds(at, 2 * hw)]
        k = qkv_o[:, pl.ds(pl.multiple_of(d + at, 2 * hw), 2 * hw)]
        v = qkv_o[:, pl.ds(pl.multiple_of(2 * d + at, 2 * hw), 2 * hw)]
        outs = []
        tops = []
        for e in range(2):
            mine = (lane < hw) if e == 0 else (lane >= hw)
            spare = lane == hw * (1 - e)
            one = jnp.where(spare, 1.0, 0.0).astype(BF16)
            qm = jnp.where(mine, q, one)
            km = jnp.where(spare, bias, k)
            s = dot_nt(qm, km)
            top = jnp.max(s, axis=-1, keepdims=True)
            pr = jnp.exp2((s - top) * scale2).astype(BF16)
            vm = jnp.where(mine, v, jnp.ones_like(v))
            outs.append(dot_nn(pr, vm))
            tops.append(top)
        low = lane < hw
        total = pltpu.roll(jnp.where(low, outs[1], outs[0]), hw, 1)
        att_o[:, pl.ds(at, 2 * hw)] = (jnp.where(low, outs[0], outs[1]) / total).astype(BF16)
        log_total = jnp.log2(total) + scale2 * jnp.where(low, tops[0], tops[1])
        first = jnp.broadcast_to(log_total[:, 0:1], (rows, 128))
        second = jnp.broadcast_to(log_total[:, hw : hw + 1], (rows, 128))
        lse_s[...] = jnp.where(
            head_lane == 2 * p, first, jnp.where(head_lane == 2 * p + 1, second, lse_s[...])
        )
        return carry

    lax.fori_loop(0, HEADS // 2, pair, 0)
    lse_o[...] = jnp.transpose(lse_s[...])[0:16, :]
    branch = dot_nn(att_o[...], wproj[...]) + vec[4:5, :]
    for i in range(pieces):
        part = slice(i * rp, (i + 1) * rp)
        middle = xs[i][...].astype(F32) + branch[part, :]
        mid_o[part, :] = middle
        xhat, _ = norm_stats(middle)
        n2_o[part, :] = (xhat * vec[1:2, :] + vec[7:8, :]).astype(BF16)


def attn_fwd(c, info, own, others, vec, wqkv, wproj, held):
    cpd, rp, d = own.shape
    pieces = 1 + len(others)
    rows = rp * pieces
    whole = lambda a: pl.BlockSpec(a.shape, lambda i, s: (0,) * a.ndim)
    at_clip = lambda shape: pl.BlockSpec((None,) + shape, lambda i, s: (c, 0, 0))
    shapes = [
        ((rows, d), BF16),
        ((rows, 3 * d), BF16),
        ((rows, d), BF16),
        ((16, rows), F32),
        ((rows, d), F32),
        ((rows, d), BF16),
    ]
    in_specs = [at_clip((rp, d))] + [whole(o) for o in others] + [whole(vec), whole(wqkv), whole(wproj)]
    operands = [own, *others, vec, wqkv, wproj]
    aliases = {}
    if held is not None:
        aliases = {1 + len(operands) + i: i for i in range(6)}
        in_specs = in_specs + [pl.BlockSpec(memory_space=pl.ANY)] * 6
        operands = operands + list(held)
    return pl.pallas_call(
        functools.partial(attn_fwd_kernel, c, pieces),
        grid_spec=pltpu.PrefetchScalarGridSpec(
            num_scalar_prefetch=1,
            grid=(1,),
            in_specs=in_specs,
            out_specs=[at_clip(s) for s, _ in shapes],
            scratch_shapes=[pltpu.VMEM((rows, 128), F32)],
        ),
        out_shape=[jax.ShapeDtypeStruct((cpd,) + s, t) for s, t in shapes],
        input_output_aliases=aliases,
        compiler_params=pltpu.CompilerParams(vmem_limit_bytes=48 * MIB),
        cost_estimate=pl.CostEstimate(
            flops=2 * rows * d * 4 * d + 16 * HEADS * rows * rows * (d // HEADS),
            bytes_accessed=rows * d * 16 + 8 * d * d,
            transcendentals=HEADS * rows * rows,
        ),
        name="attn_fwd",
    )(info, *operands)


def mlp_fwd_kernel(pieces, info, mid, n2, vec, w1, b1, w2, *outs):
    h_o = outs[pieces]
    rows, d = n2.shape
    rp = rows // pieces
    full = info[1 + pl.program_id(0)] == 1
    ff = w1.shape[1]
    chunk = d
    x = n2[...]
    acc = mid[...] + vec[5:6, :]
    for j in range(ff // chunk):
        part = slice(j * chunk, (j + 1) * chunk)
        h = dot_nn(x, w1[:, part]) + b1[:, part]
        h_o[:, part] = h.astype(BF16)
        act = (h * (0.5 + 0.5 * lax.erf(h * 0.7071067811865476))).astype(BF16)
        acc = acc + dot_nn(act, w2[part, :])
    out = jnp.where(row_valid(rows, rp, full), acc, 0.0).astype(BF16)
    for i in range(pieces):
        outs[i][...] = out[i * rp : (i + 1) * rp, :]


def mlp_fwd(info, mid, n2, vec, w1, b1, w2, clips, pieces):
    cpd, rows, d = n2.shape
    ff = w1.shape[1]
    rp = rows // pieces
    by_clip = lambda w: pl.BlockSpec((None, rows, w), lambda c, s: (c, 0, 0))
    once = lambda a: pl.BlockSpec(a.shape, lambda c, s: (0, 0), pipeline_mode=pl.Buffered(1))
    return pl.pallas_call(
        functools.partial(mlp_fwd_kernel, pieces),
        grid_spec=pltpu.PrefetchScalarGridSpec(
            num_scalar_prefetch=1,
            grid=(cpd,),
            in_specs=[by_clip(d), by_clip(d), once(vec), once(w1), once(b1), once(w2)],
            out_specs=[pl.BlockSpec((None, rp, d), lambda c, s: (s[0] * cpd + c, 0, 0))]
            + [pl.BlockSpec((None, rp, d), lambda c, s: (c, 0, 0))] * (pieces - 1)
            + [by_clip(ff)],
        ),
        out_shape=[jax.ShapeDtypeStruct((clips, rp, d), BF16)]
        + [jax.ShapeDtypeStruct((cpd, rp, d), BF16)] * (pieces - 1)
        + [jax.ShapeDtypeStruct((cpd, rows, ff), BF16)],
        compiler_params=pltpu.CompilerParams(vmem_limit_bytes=56 * MIB),
        cost_estimate=pl.CostEstimate(
            flops=4 * cpd * rows * d * ff,
            bytes_accessed=cpd * rows * (8 * d + 2 * ff) + 4 * d * ff,
            transcendentals=cpd * rows * ff,
        ),
        name="mlp_fwd",
    )(info, mid, n2, vec, w1, b1, w2)


def upstream_of(cots, full):
    rp = cots[0].shape[0]
    keep = row_valid(rp, rp, full)
    return jnp.concatenate(
        [jnp.where(keep, c[...].astype(F32), 0.0) for c in cots], axis=0
    )


def mlp_back_hidden_kernel(pieces, info, *refs):
    cots = refs[:pieces]
    h, w2, dh_o, gw2_o, sums_o, fc1_sums_o, acc = refs[pieces:]
    r = pl.program_id(0)
    last = pl.num_programs(0) - 1
    up = upstream_of(cots, info[1 + r] == 1)
    up_low = up.astype(BF16)
    ff, d = w2.shape
    chunk = d

    @pl.when(r == 0)
    def _():
        acc[...] = jnp.zeros_like(acc)
        sums_o[...] = jnp.zeros_like(sums_o)
        fc1_sums_o[...] = jnp.zeros_like(fc1_sums_o)

    sums_o[0:1, :] += jnp.sum(up, axis=0, keepdims=True)
    for j in range(ff // chunk):
        part = slice(j * chunk, (j + 1) * chunk)
        pre = h[:, part].astype(F32)
        cdf = 0.5 + 0.5 * lax.erf(pre * 0.7071067811865476)
        density = 0.3989422804014327 * jnp.exp2(pre * pre * (-0.5 * LOG2E))
        act = (pre * cdf).astype(BF16)
        grad = dot_nt(up_low, w2[part, :])
        dh = (grad * (cdf + pre * density)).astype(BF16)
        dh_o[:, part] = dh
        fc1_sums_o[0:1, part] += jnp.sum(dh.astype(F32), axis=0, keepdims=True)
        acc[part, :] += dot_tn(act, up_low)

    @pl.when(r == last)
    def _():
        gw2_o[...] = acc[...].astype(BF16)


def mlp_back_hidden(info, cot, cot_others, h, w2):
    clips, rp, d = cot.shape
    cpd, rows, ff = h.shape
    pieces = 1 + len(cot_others)
    once = lambda a: pl.BlockSpec(a.shape, lambda c, s: (0, 0), pipeline_mode=pl.Buffered(1))
    held = lambda shape: pl.BlockSpec(shape, lambda c, s: (0, 0))
    return pl.pallas_call(
        functools.partial(mlp_back_hidden_kernel, pieces),
        grid_spec=pltpu.PrefetchScalarGridSpec(
            num_scalar_prefetch=1,
            grid=(cpd,),
            in_specs=[pl.BlockSpec((None, rp, d), lambda c, s: (s[0] * cpd + c, 0, 0))]
            + [pl.BlockSpec((None, rp, d), lambda c, s: (c, 0, 0))] * (pieces - 1)
            + [pl.BlockSpec((None, rows, ff), lambda c, s: (c, 0, 0)), once(w2)],
            out_specs=[
                pl.BlockSpec((None, rows, ff), lambda c, s: (c, 0, 0)),
                held((ff, d)),
                held((8, d)),
                held((8, ff)),
            ],
            scratch_shapes=[pltpu.VMEM((ff, d), F32)],
        ),
        out_shape=[
            jax.ShapeDtypeStruct((cpd, rows, ff), BF16),
            jax.ShapeDtypeStruct((ff, d), BF16),
            jax.ShapeDtypeStruct((8, d), F32),
            jax.ShapeDtypeStruct((8, ff), F32),
        ],
        compiler_params=pltpu.CompilerParams(vmem_limit_bytes=60 * MIB),
        cost_estimate=pl.CostEstimate(
            flops=4 * cpd * rows * d * ff,
            bytes_accessed=cpd * rows * (2 * d + 4 * ff) + 4 * d * ff,
            transcendentals=2 * cpd * rows * ff,
        ),
        name="mlp_back_hidden",
    )(info, cot, *cot_others, h, w2)


def mlp_back_input_kernel(pieces, info, *refs):
    cots = refs[:pieces]
    dh, n2, mid, vec, w1, dmid_o, gw1_o, sums_o, acc = refs[pieces:]
    r = pl.program_id(0)
    last = pl.num_programs(0) - 1

    @pl.when(r == 0)
    def _():
        acc[...] = jnp.zeros_like(acc)
        sums_o[...] = jnp.zeros_like(sums_o)

    d, ff = w1.shape
    chunk = d
    x = n2[...]
    dn2 = jnp.zeros(mid.shape, F32)
    for j in range(ff // chunk):
        part = slice(j * chunk, (j + 1) * chunk)
        piece = dh[:, part]
        dn2 = dn2 + dot_nt(piece, w1[:, part])
        acc[:, part] += dot_tn(x, piece)
    dx, gain, shift = norm_back(dn2, mid[...], vec[1:2, :])
    dmid = upstream_of(cots, info[1 + r] == 1) + dx
    dmid_o[...] = dmid
    sums_o[0:1, :] += gain
    sums_o[1:2, :] += shift

    @pl.when(r == last)
    def _():
        gw1_o[...] = acc[...].astype(BF16)


def mlp_back_input(info, cot, cot_others, dh, n2, mid, vec, w1):
    clips, rp, d = cot.shape
    cpd, rows, ff = dh.shape
    pieces = 1 + len(cot_others)
    once = lambda a: pl.BlockSpec(a.shape, lambda c, s: (0, 0), pipeline_mode=pl.Buffered(1))
    held = lambda shape: pl.BlockSpec(shape, lambda c, s: (0, 0))
    by_clip = lambda w: pl.BlockSpec((None, rows, w), lambda c, s: (c, 0, 0))
    return pl.pallas_call(
        functools.partial(mlp_back_input_kernel, pieces),
        grid_spec=pltpu.PrefetchScalarGridSpec(
            num_scalar_prefetch=1,
            grid=(cpd,),
            in_specs=[pl.BlockSpec((None, rp, d), lambda c, s: (s[0] * cpd + c, 0, 0))]
            + [pl.BlockSpec((None, rp, d), lambda c, s: (c, 0, 0))] * (pieces - 1)
            + [by_clip(ff), by_clip(d), by_clip(d), once(vec), once(w1)],
            out_specs=[by_clip(d), held((d, ff)), held((8, d))],
            scratch_shapes=[pltpu.VMEM((d, ff), F32)],
        ),
        out_shape=[
            jax.ShapeDtypeStruct((cpd, rows, d), F32),
            jax.ShapeDtypeStruct((d, ff), BF16),
            jax.ShapeDtypeStruct((8, d), F32),
        ],
        compiler_params=pltpu.CompilerParams(vmem_limit_bytes=60 * MIB),
        cost_estimate=pl.CostEstimate(
            flops=4 * cpd * rows * d * ff,
            bytes_accessed=cpd * rows * (12 * d + 2 * ff) + 4 * d * ff,
            transcendentals=0,
        ),
        name="mlp_back_input",
    )(info, cot, *cot_others, dh, n2, mid, vec, w1)


def attn_back_kernel(c, pieces, info, *refs):
    xs = refs[:pieces]
    keep, dmid, qkv, att, lse, vec, wqkv, wproj = refs[pieces : pieces + 8]
    dqkv_o, sums_o, *gtok = refs[-5 - pieces : -3]
    do_s, delta_s, dqt_s = refs[-3:]
    rp, d = xs[0].shape
    rows = rp * pieces
    hw = d // HEADS
    full = info[1 + c] == 1
    low_mid = dmid[...].astype(BF16)
    do_s[...] = dot_nt(low_mid, wproj[...]).astype(BF16)
    prod = do_s[...].astype(F32) * att[...].astype(F32)
    high = prod.astype(BF16)
    rest = (prod - high.astype(F32)).astype(BF16)
    head_of = lax.broadcasted_iota(jnp.int32, (16, d), 1) // hw
    select = (head_of == lax.broadcasted_iota(jnp.int32, (16, d), 0)).astype(BF16)
    delta_s[...] = dot_nt(select, high) + dot_nt(select, rest)
    scale = hw**-0.5
    scale2 = scale * LOG2E
    bias = jnp.where(row_valid(rows, rp, full), 0.0, -1e30).astype(BF16)
    lane = lax.broadcasted_iota(jnp.int32, (1, 2 * hw), 1)

    def pair(p, carry):
        at = pl.multiple_of(p * 2 * hw, 2 * hw)
        q = qkv[:, pl.ds(at, 2 * hw)]
        k = qkv[:, pl.ds(pl.multiple_of(d + at, 2 * hw), 2 * hw)]
        v = qkv[:, pl.ds(pl.multiple_of(2 * d + at, 2 * hw), 2 * hw)]
        do = do_s[:, pl.ds(at, 2 * hw)]
        kt = jnp.transpose(k)
        zero = jnp.zeros_like(q)
        dk = dv = None
        for e in range(2):
            mine = (lane < hw) if e == 0 else (lane >= hw)
            spare = lane == hw * (1 - e)
            one = jnp.where(spare, 1.0, 0.0).astype(BF16)
            qm = jnp.where(mine, q, one)
            km = jnp.where(spare, bias, k)
            st = dot_nt(km, qm)
            pt = jnp.exp2(st * scale2 - lse[pl.ds(2 * p + e, 1), :])
            vm = jnp.where(mine, v, zero)
            dpt = dot_nt(vm, do)
            dst = (pt * (dpt - delta_s[pl.ds(2 * p + e, 1), :])).astype(BF16)
            dom = jnp.where(mine, do, zero)
            qz = jnp.where(mine, q, zero)
            dv_e = dot_nn(pt.astype(BF16), dom)
            dk_e = dot_nn(dst, qz)
            dv = dv_e if dv is None else dv + dv_e
            dk = dk_e if dk is None else dk + dk_e
            dqt_s[pl.ds(pl.multiple_of(at + e * hw, hw), hw), :] = dot_nn(
                kt[e * hw : (e + 1) * hw, :], dst
            )
        dqkv_o[:, pl.ds(pl.multiple_of(d + at, 2 * hw), 2 * hw)] = (dk * scale).astype(BF16)
        dqkv_o[:, pl.ds(pl.multiple_of(2 * d + at, 2 * hw), 2 * hw)] = dv.astype(BF16)
        return carry

    lax.fori_loop(0, HEADS // 2, pair, 0)
    dqkv_o[:, 0:d] = jnp.transpose((dqt_s[...] * scale).astype(BF16))
    dn1 = dot_nt(dqkv_o[...], wqkv[...])
    sums_o[...] = jnp.zeros_like(sums_o)
    sums_o[0:1, :] = jnp.sum(dqkv_o[:, 0:d].astype(F32), axis=0, keepdims=True)
    sums_o[1:2, :] = jnp.sum(dqkv_o[:, 2 * d : 3 * d].astype(F32), axis=0, keepdims=True)
    sums_o[2:3, :] = jnp.sum(low_mid.astype(F32), axis=0, keepdims=True)
    for i in range(pieces):
        part = slice(i * rp, (i + 1) * rp)
        dx, gain, shift = norm_back(dn1[part, :], xs[i][...].astype(F32), vec[0:1, :])
        entered = dmid[part, :] + dx
        kept = entered * keep[part, :]
        gtok[i][...] = kept.astype(BF16)
        sums_o[3:4, :] += gain
        sums_o[4:5, :] += shift
        sums_o[5:6, :] += jnp.sum(entered - kept, axis=0, keepdims=True)


def attn_back(c, info, own, others, keep, dmid, qkv, att, lse, vec, wqkv, wproj, held, clips):
    cpd, rp, d = own.shape
    pieces = 1 + len(others)
    rows = rp * pieces
    whole = lambda a: pl.BlockSpec(a.shape, lambda i, s: (0,) * a.ndim)
    at_clip = lambda shape: pl.BlockSpec((None,) + shape, lambda i, s: (c, 0, 0))
    in_specs = (
        [at_clip((rp, d))]
        + [whole(o) for o in others]
        + [
            at_clip((rows, 1)),
            at_clip((rows, d)),
            at_clip((rows, 3 * d)),
            at_clip((rows, d)),
            at_clip((16, rows)),
            whole(vec),
            whole(wqkv),
            whole(wproj),
        ]
    )
    operands = [own, *others, keep, dmid, qkv, att, lse, vec, wqkv, wproj]
    aliases = {}
    if held is not None:
        aliases = {1 + len(operands) + i: i for i in range(3)}
        in_specs = in_specs + [pl.BlockSpec(memory_space=pl.ANY)] * 3
        operands = operands + list(held)
    return pl.pallas_call(
        functools.partial(attn_back_kernel, c, pieces),
        grid_spec=pltpu.PrefetchScalarGridSpec(
            num_scalar_prefetch=1,
            grid=(1,),
            in_specs=in_specs,
            out_specs=[
                at_clip((rows, 3 * d)),
                at_clip((8, d)),
                pl.BlockSpec((None, rp, d), lambda i, s: (s[0] * cpd + c, 0, 0)),
            ]
            + [pl.BlockSpec((rp, d), lambda i, s: (0, 0))] * (pieces - 1),
            scratch_shapes=[
                pltpu.VMEM((rows, d), BF16),
                pltpu.VMEM((16, rows), F32),
                pltpu.VMEM((d, rows), F32),
            ],
        ),
        out_shape=[
            jax.ShapeDtypeStruct((cpd, rows, 3 * d), BF16),
            jax.ShapeDtypeStruct((cpd, 8, d), F32),
            jax.ShapeDtypeStruct((clips, rp, d), BF16),
        ]
        + [jax.ShapeDtypeStruct((rp, d), BF16)] * (pieces - 1),
        input_output_aliases=aliases,
        compiler_params=pltpu.CompilerParams(vmem_limit_bytes=56 * MIB),
        cost_estimate=pl.CostEstimate(
            flops=2 * rows * d * 4 * d + 40 * HEADS * rows * rows * (d // HEADS),
            bytes_accessed=rows * d * 28 + 8 * d * d,
            transcendentals=HEADS * rows * rows,
        ),
        name="attn_back",
    )(info, *operands)


def weight_grad_kernel(a, b, o):
    o[...] = dot_tn(a[...].astype(BF16), b[...].astype(BF16)).astype(BF16)


def weight_grad(a, b, chunk):
    rows, m = a.shape
    n = b.shape[1]
    return pl.pallas_call(
        weight_grad_kernel,
        grid=(n // chunk,),
        in_specs=[
            pl.BlockSpec((rows, m), lambda j: (0, 0), pipeline_mode=pl.Buffered(1)),
            pl.BlockSpec((rows, chunk), lambda j: (0, j)),
        ],
        out_specs=pl.BlockSpec((m, chunk), lambda j: (0, j)),
        out_shape=jax.ShapeDtypeStruct((m, n), BF16),
        compiler_params=pltpu.CompilerParams(vmem_limit_bytes=48 * MIB),
        cost_estimate=pl.CostEstimate(
            flops=2 * rows * m * n, bytes_accessed=2 * (rows * m + rows * n + m * n), transcendentals=0
        ),
        name="weight_grad",
    )(a, b)


def power_of_two(n):
    return n & (n - 1) == 0


def scatter_sum(x, wide, narrow):
    rows, cols = x.shape
    if not (power_of_two(wide) and power_of_two(narrow)):
        return lax.psum_scatter(
            x.astype(F32), ("wide", "narrow"), scatter_dimension=0, tiled=True
        )
    bits_w, bits_n = wide.bit_length() - 1, narrow.bit_length() - 1
    order = [("wide", b, bits_w - 1 - b, wide) for b in range(bits_w)]
    order += [("narrow", b, bits_w + bits_n - 1 - b, narrow) for b in range(bits_n)]
    t = x.reshape((2,) * (bits_w + bits_n) + (rows // (wide * narrow), cols))
    for step, (axis, b, dim, size) in enumerate(order):
        mine = (lax.axis_index(axis) >> b) & 1
        keep = lax.dynamic_slice_in_dim(t, mine, 1, dim)
        send = lax.dynamic_slice_in_dim(t, 1 - mine, 1, dim)
        got = lax.ppermute(send, axis, [(i, i ^ (1 << b)) for i in range(size)])
        t = keep.astype(F32) + got.astype(F32)
        if step < len(order) - 1:
            t = t.astype(BF16)
    return t.reshape(rows // (wide * narrow), cols).astype(F32)


def body(
    wide,
    narrow,
    tokens,
    masked,
    resolution,
    mask_embed,
    gains,
    biases,
    w_qkv,
    w_proj,
    w_fc1,
    fc1_bias,
    w_fc2,
    cotangent,
):
    clips, freq_rows, cols, d = tokens.shape
    rp = freq_rows * cols
    cpd = clips // narrow
    rows = rp * narrow
    ff = w_fc1.shape[1]
    me = lax.axis_index("narrow")
    flat_tokens = tokens.reshape(clips, rp, d)
    flat_cot = cotangent.reshape(clips, rp, d)
    is_masked = masked.reshape(clips, rp) == 1

    def block_of(array, rank, at, count):
        return lax.dynamic_slice_in_dim(array, rank * cpd + at, count, 0)

    def entered_of(rank, at, count):
        return jnp.where(
            block_of(is_masked, rank, at, count)[:, :, None],
            mask_embed[None, None, :],
            block_of(flat_tokens, rank, at, count),
        )

    def to_rank(array, k):
        return lax.ppermute(array, "narrow", [(i, (i + k) % narrow) for i in range(narrow)])

    def from_rank(array, k):
        return lax.ppermute(array, "narrow", [(i, (i - k) % narrow) for i in range(narrow)])

    info = jnp.concatenate([me[None].astype(jnp.int32), block_of(resolution, me, 0, cpd)])
    vec = jnp.concatenate([gains.astype(F32).T, biases.astype(F32).T], axis=0)
    bias_row = fc1_bias.astype(F32)[None, :]

    shifts = range(1, narrow)
    others = [
        [to_rank(entered_of((me + k) % narrow, c, 1)[0], k) for k in shifts] for c in range(cpd)
    ]
    keep_cols = [block_of(masked.reshape(clips, rp), me, 0, cpd)]
    keep_cols += [to_rank(block_of(masked.reshape(clips, rp), (me + k) % narrow, 0, cpd), k) for k in shifts]
    keep = (jnp.concatenate(keep_cols, axis=1) != 1).astype(F32)[:, :, None]
    own = entered_of(me, 0, cpd)
    cot_send = [block_of(flat_cot, (me + k) % narrow, 0, cpd) for k in shifts]
    if narrow > 1:
        cot_send, others[-1] = lax.optimization_barrier((cot_send, others[-1]))
    cot_others = [to_rank(cot_send[k - 1], k) for k in shifts]

    held = None
    for c in range(cpd):
        held = attn_fwd(c, info, own, others[c], vec, w_qkv, w_proj, held)
    n1, qkv, att, lse, mid, n2 = held

    out, *rest = mlp_fwd(info, mid, n2, vec, w_fc1, bias_row, w_fc2, clips, narrow)
    out_others, h = rest[:-1], rest[-1]
    out_back = [from_rank(out_others[k - 1], k) for k in shifts]

    dh, g_fc2, up_sums, fc1_sums = mlp_back_hidden(info, flat_cot, cot_others, h, w_fc2)
    grad_fc2 = scatter_sum(g_fc2, wide, narrow)
    dmid, g_fc1, two_sums = mlp_back_input(info, flat_cot, cot_others, dh, n2, mid, vec, w_fc1)
    grad_fc1 = scatter_sum(g_fc1, wide, narrow)
    g_proj = weight_grad(att.reshape(cpd * rows, d), dmid.reshape(cpd * rows, d), d)
    grad_proj = scatter_sum(g_proj, wide, narrow)

    held = None
    tok_back = []
    for c in range(cpd):
        *held, = attn_back(
            c, info, own, others[c], keep, dmid, qkv, att, lse, vec, w_qkv, w_proj, held, clips
        )
        tok_back.append([from_rank(g, k) for k, g in zip(shifts, held[3:])])
        held = held[:3]
    dqkv, one_sums, grad_tokens = held
    one = jnp.sum(one_sums, axis=0)
    g_qkv = weight_grad(n1.reshape(cpd * rows, d), dqkv.reshape(cpd * rows, 3 * d), d)
    rows_of = jnp.concatenate(
        [
            one[5:6],
            one[3:4],
            two_sums[0:1],
            one[0:1],
            one[1:2],
            one[2:3],
            up_sums[0:1],
            one[4:5],
            two_sums[1:2],
        ],
        axis=0,
    )
    small = jnp.concatenate([rows_of.T, fc1_sums[0].reshape(d, ff // d)], axis=1)
    small = jnp.pad(small, ((0, 0), (0, -small.shape[1] % 128))).astype(BF16)
    last = scatter_sum(jnp.concatenate([g_qkv, small], axis=1), wide, narrow)
    grad_qkv = last[:, : 3 * d]
    vectors = last[:, 3 * d :]

    for k in shifts:
        rank = (me + k) % narrow
        out = lax.dynamic_update_slice_in_dim(out, out_back[k - 1], rank * cpd, 0)
    for c in range(cpd):
        for k in shifts:
            rank = (me + k) % narrow
            grad_tokens = lax.dynamic_update_slice_in_dim(
                grad_tokens, tok_back[c][k - 1][None], rank * cpd + c, 0
            )
    return (
        out.reshape(tokens.shape),
        grad_tokens.reshape(tokens.shape),
        vectors[:, 0],
        vectors[:, 1:3],
        vectors[:, 3:9],
        grad_qkv,
        grad_proj,
        grad_fc1,
        vectors[:, 9 : 9 + ff // d].reshape(-1),
        grad_fc2,
    )


def solution(mesh):
    split = P("wide", None, "narrow", None)
    every = P(("wide", "narrow"))
    rows = P(("wide", "narrow"), None)
    return jax.shard_map(
        functools.partial(body, mesh.shape["wide"], mesh.shape["narrow"]),
        mesh=mesh,
        in_specs=(split, P("wide", None, "narrow"), P("wide")) + (P(),) * 8 + (split,),
        out_specs=(split, split, every, rows, rows, rows, rows, rows, every, rows),
        check_vma=False,
    )
```

time: 1260 us -> 456 us (0.36)
  waiting for transfers between devices: 495 us -> 116 us
  matrix products: 363 us -> 0 us
  Pallas kernels: 0 us -> 254 us
  local copies, waits for them, and re-layouts: 219 us -> 22 us
  other arithmetic: 114 us -> 18.9 us
  blocking collectives: 40.9 us -> 0 us
  starting transfers between devices: 0.89 us -> 39.3 us
  between operations: 15 us -> 1.6 us
    reduce_scatter x6 -> x0, waiting for transfers between devices: 385 us -> none  [the longest x1 141 us: body(): lax.psum_scatter(grad_fc1, ('wide', 'narrow'), scatter_dimension=0, tiled...]
    dot_general x18 -> x0, matrix products: 363 us -> none  [the longest x1 69.3 us: body(): jnp.dot(low_two, w_fc1, preferred_element_type=jnp.float32)]
    pallas_call x0 -> x13, Pallas kernels: none -> 254 us  [the longest x4 79.5 us: attn_back(): pl.pallas_call(functools.partial(attn_back_kernel, c, pieces), grid_spec=...]
    ppermute x0 -> x31, waiting for transfers between devices: none -> 116 us  [the longest x20 81.5 us: scatter_sum(): got = lax.ppermute(send, axis, [(i, i ^ 1 << b) for i in range(size)])]
    all_gather x2 -> x0, waiting for transfers between devices: 110 us -> none  [the longest x1 62.2 us: body(): lax.all_gather(value_rows, 'narrow', axis=2, tiled=True)]
    convert_element_type x8 -> x0, local copies, waits for them, and re-layouts: 81.5 us -> none  [the longest x2 34.1 us: body(): value_part.reshape(full_shape).astype(jnp.bfloat16)]
    reduce_sum x10 -> x1, other arithmetic: 51.2 us -> 0.01 us  [body(): one = jnp.sum(one_sums, axis=0)]
    reshape x6 -> x2, local copies, waits for them, and re-layouts: 51 us -> 1.44 us  [the longest x1 0.83 us: body(): is_masked = masked.reshape(clips, rp) == 1]
  transfers between devices with their start and end apart: 8 -> 31, of which waited for: 6 -> 17; matrix products, arithmetic and copies ran while one was open for 28% -> 8% of each run, Pallas kernels for 0% -> 56%
where the time goes in v1:
time: 456 us; the launch traced here: 452 us
  Pallas kernels  254 us (56%)
  waiting for transfers between devices  116 us (25%)
  starting transfers between devices  39.3 us (9%)
  local copies, waits for them, and re-layouts  22 us (5%)
  other arithmetic  18.9 us (4%)
    ppermute x20, waiting for transfers between devices, scatter_sum(): got = lax.ppermute(send, axis, [(i, i ^ 1 << b) for i in range(size)])  81.5 us
    pallas_call x4, Pallas kernels, attn_back(): pl.pallas_call(functools.partial(attn_back_kernel, c, pieces), grid_spec=...  79.5 us
    pallas_call x4, Pallas kernels, attn_fwd(): pl.pallas_call(functools.partial(attn_fwd_kernel, c, pieces), grid_spec=p...  62.6 us
    pallas_call x1, Pallas kernels, mlp_back_hidden(): pl.pallas_call(functools.partial(mlp_back_hidden_kernel, pieces), grid_sp...  35.6 us
    pallas_call x1, Pallas kernels, mlp_back_input(): pl.pallas_call(functools.partial(mlp_back_input_kernel, pieces), grid_spe...  31.6 us
    ppermute x6, waiting for transfers between devices, to_rank(): lax.ppermute(array, 'narrow', [(i, (i + k) % narrow) for i in range(narro...  28 us
    pallas_call x1, Pallas kernels, mlp_fwd(): pl.pallas_call(functools.partial(mlp_fwd_kernel, pieces), grid_spec=pltpu...  27.9 us
    ppermute x20, starting transfers between devices, scatter_sum(): got = lax.ppermute(send, axis, [(i, i ^ 1 << b) for i in range(size)])  25.1 us
  transfers between devices with their start and end apart: 31, of which 17 were waited for; matrix products, arithmetic and copies ran while one was open for 8% of the time, Pallas kernels for 56%

profile of v1, /device:TPU:0, one launch (start us, length us, event | category | flops | bytes accessed | tf_op | source)
XLA Modules:
  0.0 452.3 jit_solution(1563714630662344068)
XLA Ops:
  1.5 3.0 collective-permute-start.5
  15.5 28.0 %collective-permute-done.refs_1_ = bf16[256,768]{1,0:T(8,128)(2,1)S(1)} collective-permute-done((bf16[256,768]{1,0:T(8,128)(2,1)}, bf16[256,768]{1,0:T(8,128)(2,1)S(1)}, u32[]{:S(2)}, u32[]{:S(2)}) %collective-permute-start) | collective-permute-done | bytes 393248 | tf_op jit(solution)/shard_map/ppermute | solution.py:568
  43.9 17.2 %attn_fwd.4 = (bf16[4,512,768]{2,1,0:T(8,128)(2,1)}, bf16[4,512,2304]{2,1,0:T(8,128)(2,1)}, bf16[4,512,768]{2,1,0:T(8,128)(2,1)}, f32[4,16,512]{2,1,0:T(8,128)S(...) custom-call(s32[5]{0:T(128)S(1)} %pad_add_fusion.info, ...), custom_call_target="tpu_custom_call" | custom-call | flops 5637144576 | bytes 11010048 | tf_op jit(solution)/shard_map/attn_fwd/pallas_call | solution.py:134
  61.0 15.1 %attn_fwd.5 = (bf16[4,512,768]{2,1,0:T(8,128)(2,1)}, bf16[4,512,2304]{2,1,0:T(8,128)(2,1)}, bf16[4,512,768]{2,1,0:T(8,128)(2,1)}, f32[4,16,512]{2,1,0:T(8,128)S(...) custom-call(s32[5]{0:T(128)S(1)} %pad_add_fusion.info, ...), custom_call_target="tpu_custom_call", output_to_operand_aliasing={{0}: (6, {}), {1}: (7, {}), {2}: (8, {}), {3}: (9, {}), {4}... | custom-call | flops 5637144576 | bytes 11010048 | tf_op jit(solution)/shard_map/attn_fwd/pallas_call | solution.py:134
  76.2 15.3 %attn_fwd.6 = (bf16[4,512,768]{2,1,0:T(8,128)(2,1)}, bf16[4,512,2304]{2,1,0:T(8,128)(2,1)}, bf16[4,512,768]{2,1,0:T(8,128)(2,1)}, f32[4,16,512]{2,1,0:T(8,128)S(...) custom-call(s32[5]{0:T(128)S(1)} %pad_add_fusion.info, ...), custom_call_target="tpu_custom_call", output_to_operand_aliasing={{0}: (6, {}), {1}: (7, {}), {2}: (8, {}), {3}: (9, {}), {4}... | custom-call | flops 5637144576 | bytes 11010048 | tf_op jit(solution)/shard_map/attn_fwd/pallas_call | solution.py:134
  91.5 15.0 %attn_fwd.7 = (bf16[4,512,768]{2,1,0:T(8,128)(2,1)}, bf16[4,512,2304]{2,1,0:T(8,128)(2,1)}, bf16[4,512,768]{2,1,0:T(8,128)(2,1)}, f32[4,16,512]{2,1,0:T(8,128)S(...) custom-call(s32[5]{0:T(128)S(1)} %pad_add_fusion.info, ...), custom_call_target="tpu_custom_call", output_to_operand_aliasing={{0}: (6, {}), {1}: (7, {}), {2}: (8, {}), {3}: (9, {}), {4}... | custom-call | flops 5637144576 | bytes 11010048 | tf_op jit(solution)/shard_map/attn_fwd/pallas_call | solution.py:134
  106.5 27.9 %mlp_fwd.1 = (bf16[8,256,768]{2,1,0:T(8,128)(2,1)}, bf16[4,256,768]{2,1,0:T(8,128)(2,1)}, bf16[4,512,3072]{2,1,0:T(8,128)(2,1)}) custom-call(s32[5]{0:T(128)} %copy-done.9, f32[4,512,768]{2,1,0:T(8,128)} %get-tuple-element.81.mid.refs_4_, bf16[4,512,768]{2,1,0:T(8,128)(2,1)} %get-tuple-element.82.n2.refs_3_, f32[8,768]{1,0:T(8,128)} %copy-done.8, ...), custom_call_target="tpu_custom_call" | custom-call | flops 19327352832 | bytes 34603008 | tf_op jit(solution)/shard_map/mlp_fwd/pallas_call | solution.py:181
  136.2 35.6 %mlp_back_hidden.1 = (bf16[4,512,3072]{2,1,0:T(8,128)(2,1)}, bf16[3072,768]{1,0:T(8,128)(2,1)}, f32[8,768]{1,0:T(8,128)}, f32[8,3072]{1,0:T(8,128)}) custom-call(s32[5]{0:T(128)} %copy-done.9, bf16[8,256,768]{2,1,0:T(8,128)(2,1)} %bitcast.64, bf16[4,256,768]{2,1,0:T(8,128)(2,1)} %collective-permute-done.6.refs_1_, ...), custom_call_target="tpu_custom_call" | custom-call | flops 19327352832 | bytes 37748736 | tf_op jit(solution)/shard_map/mlp_back_hidden/pallas_call | solution.py:252
  171.9 31.6 %mlp_back_input.1 = (f32[4,512,768]{2,1,0:T(8,128)}, bf16[768,3072]{1,0:T(8,128)(2,1)}, f32[8,768]{1,0:T(8,128)}) custom-call(s32[5]{0:T(128)} %copy-done.9, bf16[8,256,768]{2,1,0:T(8,128)(2,1)} %bitcast.65, bf16[4,256,768]{2,1,0:T(8,128)(2,1)} %collective-permute-done.6.refs_1_, bf16[4,512,3072]{2,1,0:T(8,128)(2,1)} %get-tuple-element.87.refs_2_, ...), custom_call_target="tpu_custom_call" | custom-call | flops 19327352832 | bytes 40894464 | tf_op jit(solution)/shard_map/mlp_back_input/pallas_call | solution.py:322
  203.5 5.6 %weight_grad.3 = bf16[768,768]{1,0:T(8,128)(2,1)S(1)} custom-call(bf16[2048,768]{1,0:T(8,128)(2,1)S(1)} %bitcast.44, f32[2048,768]{1,0:T(8,128)} %bitcast.48), custom_call_target="tpu_custom_call" | custom-call | flops 2415919104 | bytes 7471104 | tf_op jit(solution)/shard_map/weight_grad/pallas_call | solution.py:489
  214.8 19.9 %attn_back.4 = (bf16[4,512,2304]{2,1,0:T(8,128)(2,1)}, f32[4,8,768]{2,1,0:T(8,128)}, bf16[8,256,768]{2,1,0:T(8,128)(2,1)}, bf16[256,768]{1,0:T(8,128)(2,1)}) custom-call(s32[5]{0:T(128)} %copy-done.9, bf16[4,256,768]{2,1,0:T(8,128)(2,1)} %copy-done.1, bf16[256,768]{1,0:T(8,128)(2,1)} %collective-permute-done.3.refs_1_, ...), custom_call_target="tpu_custom_call" | custom-call | flops 10468982784 | bytes 15728640 | tf_op jit(solution)/shard_map/attn_back/pallas_call | solution.py:447
  235.1 19.7 %attn_back.5 = (bf16[4,512,2304]{2,1,0:T(8,128)(2,1)}, f32[4,8,768]{2,1,0:T(8,128)}, bf16[8,256,768]{2,1,0:T(8,128)(2,1)}, bf16[256,768]{1,0:T(8,128)(2,1)}) custom-call(s32[5]{0:T(128)} %copy-done.9, bf16[4,256,768]{2,1,0:T(8,128)(2,1)} %copy-done.1, ...), custom_call_target="tpu_custom_call", output_to_operand_aliasing={{0}: (11, {}), {1}: (12, {}), {2}: (13, {})} | custom-call | flops 10468982784 | bytes 15728640 | tf_op jit(solution)/shard_map/attn_back/pallas_call | solution.py:447
  254.8 19.9 %attn_back.6 = (bf16[4,512,2304]{2,1,0:T(8,128)(2,1)}, f32[4,8,768]{2,1,0:T(8,128)}, bf16[8,256,768]{2,1,0:T(8,128)(2,1)}, bf16[256,768]{1,0:T(8,128)(2,1)}) custom-call(s32[5]{0:T(128)} %copy-done.9, bf16[4,256,768]{2,1,0:T(8,128)(2,1)} %copy-done.1, ...), custom_call_target="tpu_custom_call", output_to_operand_aliasing={{0}: (11, {}), {1}: (12, {}), {2}: (13, {})} | custom-call | flops 10468982784 | bytes 15728640 | tf_op jit(solution)/shard_map/attn_back/pallas_call | solution.py:447
  274.7 20.0 %attn_back.7 = (bf16[4,512,2304]{2,1,0:T(8,128)(2,1)}, f32[4,8,768]{2,1,0:T(8,128)}, bf16[8,256,768]{2,1,0:T(8,128)(2,1)}, bf16[256,768]{1,0:T(8,128)(2,1)}) custom-call(s32[5]{0:T(128)} %copy-done.9, bf16[4,256,768]{2,1,0:T(8,128)(2,1)} %copy-done.1, bf16[256,768]{1,0:T(8,128)(2,1)} %copy-done.7, ...), custom_call_target="tpu_custom_call", output_to_operand_aliasing={{0}: (11, {}), {1}: (12, {}), {2}: (13, {})} | custom-call | flops 10468982784 | bytes 15728640 | tf_op jit(solution)/shard_map/attn_back/pallas_call | solution.py:447
  294.7 11.3 %weight_grad.2 = bf16[768,2304]{1,0:T(8,128)(2,1)} custom-call(bf16[2048,768]{1,0:T(8,128)(2,1)S(1)} %bitcast.45, bf16[2048,2304]{1,0:T(8,128)(2,1)} %bitcast.49), custom_call_target="tpu_custom_call" | custom-call | flops 7247757312 | bytes 16121856 | tf_op jit(solution)/shard_map/weight_grad/pallas_call | solution.py:489
  324.1 5.0 %collective-permute-done.8 = bf16[256,768]{1,0:T(8,128)(2,1)S(1)} collective-permute-done((bf16[256,768]{1,0:T(8,128)(2,1)S(1)}, bf16[256,768]{1,0:T(8,128)(2,1)S(1)}, u32[]{:S(2)}, u32[]{:S(2)}) %collective-permute-start.8) | collective-permute-done | bytes 393248 | tf_op jit(solution)/shard_map/ppermute | solution.py:571
  351.5 17.2 %collective-permute-done.12 = bf16[2,2,1,1,2,24,2432]{6,5,4,3,2,1,0:T(8,128)(2,1)S(1)} collective-permute-done((bf16[2,2,1,1,2,24,2432]{6,5,4,3,2,1,0:T(8,128)(2,1)S(1)}, bf16[2,2,1,1,2,24,2432]{6,5,4,3,2,1,0:T(8,128)(2,1)S(1)}, u32[]{:S(2)}, u32[]{:S(2)}) %collective-permute-start.12) | collective-permute-done | bytes 933920 | tf_op jit(solution)/shard_map/ppermute | solution.py:524
  371.6 7.3 %collective-permute-done.13 = bf16[2,1,1,1,2,24,2432]{6,5,4,3,2,1,0:T(8,128)(2,1)S(1)} collective-permute-done((bf16[2,1,1,1,2,24,2432]{6,5,4,3,2,1,0:T(8,128)(2,1)S(1)}, bf16[2,1,1,1,2,24,2432]{6,5,4,3,2,1,0:T(8,128)(2,1)S(1)}, u32[]{:S(2)}, u32[]{:S(2)}) %collective-permute-start.13) | collective-permute-done | bytes 466976 | tf_op jit(solution)/shard_map/ppermute | solution.py:524
  382.5 6.1 %collective-permute-done.14 = bf16[1,1,1,1,2,24,2432]{6,5,4,3,2,1,0:T(8,128)(2,1)S(1)} collective-permute-done((bf16[1,1,1,1,2,24,2432]{6,5,4,3,2,1,0:T(8,128)(2,1)S(1)}, bf16[1,1,1,1,2,24,2432]{6,5,4,3,2,1,0:T(8,128)(2,1)S(1)}, u32[]{:S(2)}, u32[]{:S(2)}) %collective-permute-start.14) | collective-permute-done | bytes 233504 | tf_op jit(solution)/shard_map/ppermute | solution.py:524
  389.4 4.6 %collective-permute-done.27 = bf16[2,2,1,1,2,96,768]{6,5,4,3,2,1,0:T(8,128)(2,1)S(1)} collective-permute-done((bf16[2,2,1,1,2,96,768]{6,5,4,3,2,1,0:T(8,128)(2,1)S(1)}, bf16[2,2,1,1,2,96,768]{6,5,4,3,2,1,0:T(8,128)(2,1)S(1)}, u32[]{:S(2)}, u32[]{:S(2)}) %collective-permute-start.27) | collective-permute-done | bytes 1179680 | tf_op jit(solution)/shard_map/ppermute | solution.py:524
  396.0 17.7 %collective-permute-done.22 = bf16[2,2,1,1,2,24,3072]{6,5,4,3,2,1,0:T(8,128)(2,1)S(1)} collective-permute-done((bf16[2,2,1,1,2,24,3072]{6,5,4,3,2,1,0:T(8,128)(2,1)S(1)}, bf16[2,2,1,1,2,24,3072]{6,5,4,3,2,1,0:T(8,128)(2,1)S(1)}, u32[]{:S(2)}, u32[]{:S(2)}) %collective-permute-start.22) | collective-permute-done | bytes 1179680 | tf_op jit(solution)/shard_map/ppermute | solution.py:524
  421.5 3.1 collective-permute-start.29
  424.7 6.9 %collective-permute-done.23 = bf16[2,1,1,1,2,24,3072]{6,5,4,3,2,1,0:T(8,128)(2,1)} collective-permute-done((bf16[2,1,1,1,2,24,3072]{6,5,4,3,2,1,0:T(8,128)(2,1)}, bf16[2,1,1,1,2,24,3072]{6,5,4,3,2,1,0:T(8,128)(2,1)}, u32[]{:S(2)}, u32[]{:S(2)}) %collective-permute-start.23) | collective-permute-done | bytes 589856 | tf_op jit(solution)/shard_map/ppermute | solution.py:524
  434.8 8.0 %collective-permute-done.29 = bf16[1,1,1,1,2,96,768]{6,5,4,3,2,1,0:T(8,128)(2,1)S(1)} collective-permute-done((bf16[1,1,1,1,2,96,768]{6,5,4,3,2,1,0:T(8,128)(2,1)S(1)}, bf16[1,1,1,1,2,96,768]{6,5,4,3,2,1,0:T(8,128)(2,1)S(1)}, u32[]{:S(2)}, u32[]{:S(2)}) %collective-permute-start.29) | collective-permute-done | bytes 294944 | tf_op jit(solution)/shard_map/ppermute | solution.py:524
  (192 shorter events, 89.4 us)
Async XLA Ops:
  1.5 12.4 %collective-permute-start.5 = (s32[4,256]{1,0:T(4,128)S(1)}, s32[4,256]{1,0:T(4,128)S(1)}, u32[]{:S(2)}, u32[]{:S(2)}) collective-permute-start(s32[4,256]{1,0:T(4,128)S(1)} %get-tuple-element.178), channel_id=1, source_target_pairs={{0,1},{1,0},{2,3},{3,2},{4,5},{5,4},{6,7},{7,6},{8,9},{9,8},{10,11... | collective-permute-start | bytes 12296 | tf_op jit(solution)/shard_map/ppermute | solution.py:568
  7.5 36.4 %collective-permute-start.3 = (bf16[256,768]{1,0:T(8,128)(2,1)}, bf16[256,768]{1,0:T(8,128)(2,1)}, u32[]{:S(2)}, u32[]{:S(2)}) collective-permute-start(bf16[256,768]{1,0:T(8,128)(2,1)} %get-tuple-element.168), channel_id=1, source_target_pairs={{0,1},{1,0},{2,3},{3,2},{4,5},{5,4},{6,7},{7,6},{8,9},{9,8},{10,11... | collective-permute-start | bytes 1179656 | tf_op jit(solution)/shard_map/ppermute | solution.py:568
  7.5 53.5 %collective-permute-start.2 = (bf16[256,768]{1,0:T(8,128)(2,1)}, bf16[256,768]{1,0:T(8,128)(2,1)}, u32[]{:S(2)}, u32[]{:S(2)}) collective-permute-start(bf16[256,768]{1,0:T(8,128)(2,1)} %get-tuple-element.169), channel_id=1, source_target_pairs={{0,1},{1,0},{2,3},{3,2},{4,5},{5,4},{6,7},{7,6},{8,9},{9,8},{10,11... | collective-permute-start | bytes 1179656 | tf_op jit(solution)/shard_map/ppermute | solution.py:568
  9.5 66.7 %collective-permute-start.1 = (bf16[256,768]{1,0:T(8,128)(2,1)}, bf16[256,768]{1,0:T(8,128)(2,1)}, u32[]{:S(2)}, u32[]{:S(2)}) collective-permute-start(bf16[256,768]{1,0:T(8,128)(2,1)} %get-tuple-element.170), channel_id=1, source_target_pairs={{0,1},{1,0},{2,3},{3,2},{4,5},{5,4},{6,7},{7,6},{8,9},{9,8},{10,11... | collective-permute-start | bytes 1179656 | tf_op jit(solution)/shard_map/ppermute | solution.py:568
  9.6 34.0 %collective-permute-start = (bf16[256,768]{1,0:T(8,128)(2,1)}, bf16[256,768]{1,0:T(8,128)(2,1)S(1)}, u32[]{:S(2)}, u32[]{:S(2)}) collective-permute-start(bf16[256,768]{1,0:T(8,128)(2,1)} %get-tuple-element.171), channel_id=1, source_target_pairs={{0,1},{1,0},{2,3},{3,2},{4,5},{5,4},{6,7},{7,6},{8,9},{9,8},{10,11... | collective-permute-start | bytes 1179656 | tf_op jit(solution)/shard_map/ppermute | solution.py:568
  43.5 92.7 %collective-permute-start.6 = (bf16[4,256,768]{2,1,0:T(8,128)(2,1)}, bf16[4,256,768]{2,1,0:T(8,128)(2,1)}, u32[]{:S(2)}, u32[]{:S(2)}) collective-permute-start(bf16[4,256,768]{2,1,0:T(8,128)(2,1)} %constant_dynamic-slice_fusion.26), channel_id=1, source_target_pairs={{0,1},{1,0},{2,3},{3,2},{4,5},{5,4},{6,7},{7,6},{8,9},{9,8},{10,11... | collective-permute-start | bytes 4718600 | tf_op jit(solution)/shard_map/ppermute | solution.py:568
  134.5 179.1 %collective-permute-start.4 = (bf16[4,256,768]{2,1,0:T(8,128)(2,1)}, bf16[4,256,768]{2,1,0:T(8,128)(2,1)}, u32[]{:S(2)}, u32[]{:S(2)}) collective-permute-start(bf16[4,256,768]{2,1,0:T(8,128)(2,1)} %get-tuple-element.84), channel_id=1, source_target_pairs={{0,1},{1,0},{2,3},{3,2},{4,5},{5,4},{6,7},{7,6},{8,9},{9,8},{10,11... | collective-permute-start | bytes 4718600 | tf_op jit(solution)/shard_map/ppermute | solution.py:571
  209.2 101.9 %collective-permute-start.16 = (bf16[2,2,2,1,2,24,768]{6,5,4,3,2,1,0:T(8,128)(2,1)S(1)}, bf16[2,2,2,1,2,24,768]{6,5,4,3,2,1,0:T(8,128)(2,1)}, u32[]{:S(2)}, u32[]{:S(2)}) collective-permute-start(bf16[2,2,2,1,2,24,768]{6,5,4,3,2,1,0:T(8,128)(2,1)S(1)} %constant_dynamic-slice_fusion.14), channel_id=1, source_target_pairs={{0,2},{2,0},{4,6},{6,4},{8,10},{10,8},{12,14},{14,12},{16,18},{18,... | collective-permute-start | bytes 1769480 | tf_op jit(solution)/shard_map/ppermute | solution.py:524
  214.3 133.2 %collective-permute-start.26 = (bf16[2,2,2,1,2,96,768]{6,5,4,3,2,1,0:T(8,128)(2,1)}, bf16[2,2,2,1,2,96,768]{6,5,4,3,2,1,0:T(8,128)(2,1)}, u32[]{:S(2)}, u32[]{:S(2)}) collective-permute-start(bf16[2,2,2,1,2,96,768]{6,5,4,3,2,1,0:T(8,128)(2,1)} %constant_dynamic-slice_fusion.4), channel_id=1, source_target_pairs={{0,2},{2,0},{4,6},{6,4},{8,10},{10,8},{12,14},{14,12},{16,18},{18,... | collective-permute-start | bytes 7077896 | tf_op jit(solution)/shard_map/ppermute | solution.py:524
  214.3 156.3 %collective-permute-start.21 = (bf16[2,2,2,1,2,24,3072]{6,5,4,3,2,1,0:T(8,128)(2,1)}, bf16[2,2,2,1,2,24,3072]{6,5,4,3,2,1,0:T(8,128)(2,1)S(1)}, u32[]{:S(2)}, u32[]{:S(2)}) collective-permute-start(bf16[2,2,2,1,2,24,3072]{6,5,4,3,2,1,0:T(8,128)(2,1)} %constant_dynamic-slice_fusion.9), channel_id=1, source_target_pairs={{0,2},{2,0},{4,6},{6,4},{8,10},{10,8},{12,14},{14,12},{16,18},{18,... | collective-permute-start | bytes 7077896 | tf_op jit(solution)/shard_map/ppermute | solution.py:524
  234.7 82.3 %collective-permute-start.7 = (bf16[256,768]{1,0:T(8,128)(2,1)}, bf16[256,768]{1,0:T(8,128)(2,1)}, u32[]{:S(2)}, u32[]{:S(2)}) collective-permute-start(bf16[256,768]{1,0:T(8,128)(2,1)} %get-tuple-element.102), channel_id=1, source_target_pairs={{0,1},{1,0},{2,3},{3,2},{4,5},{5,4},{6,7},{7,6},{8,9},{9,8},{10,11... | collective-permute-start | bytes 1179656 | tf_op jit(solution)/shard_map/ppermute | solution.py:571
  311.0 33.4 %collective-permute-start.11 = (bf16[2,2,2,1,2,24,2432]{6,5,4,3,2,1,0:T(8,128)(2,1)S(1)}, bf16[2,2,2,1,2,24,2432]{6,5,4,3,2,1,0:T(8,128)(2,1)S(1)}, u32[]{:S(2)}, u32[]{:S(2)}) collective-permute-start(bf16[2,2,2,1,2,24,2432]{6,5,4,3,2,1,0:T(8,128)(2,1)S(1)} %constant_dynamic-slice_fusion.19), channel_id=1, source_target_pairs={{0,2},{2,0},{4,6},{6,4},{8,10},{10,8},{12,14},{14,12},{16,18},{18,... | collective-permute-start | bytes 5603336 | tf_op jit(solution)/shard_map/ppermute | solution.py:524
  317.0 12.1 %collective-permute-start.8 = (bf16[256,768]{1,0:T(8,128)(2,1)S(1)}, bf16[256,768]{1,0:T(8,128)(2,1)S(1)}, u32[]{:S(2)}, u32[]{:S(2)}) collective-permute-start(bf16[256,768]{1,0:T(8,128)(2,1)S(1)} %copy-done.24), channel_id=1, source_target_pairs={{0,1},{1,0},{2,3},{3,2},{4,5},{5,4},{6,7},{7,6},{8,9},{9,8},{10,11... | collective-permute-start | bytes 1179656 | tf_op jit(solution)/shard_map/ppermute | solution.py:571
  322.3 15.3 %collective-permute-start.9 = (bf16[256,768]{1,0:T(8,128)(2,1)S(1)}, bf16[256,768]{1,0:T(8,128)(2,1)S(1)}, u32[]{:S(2)}, u32[]{:S(2)}) collective-permute-start(bf16[256,768]{1,0:T(8,128)(2,1)S(1)} %copy-done.23), channel_id=1, source_target_pairs={{0,1},{1,0},{2,3},{3,2},{4,5},{5,4},{6,7},{7,6},{8,9},{9,8},{10,11... | collective-permute-start | bytes 1179656 | tf_op jit(solution)/shard_map/ppermute | solution.py:571
  334.3 11.3 %collective-permute-start.10 = (bf16[256,768]{1,0:T(8,128)(2,1)S(1)}, bf16[256,768]{1,0:T(8,128)(2,1)S(1)}, u32[]{:S(2)}, u32[]{:S(2)}) collective-permute-start(bf16[256,768]{1,0:T(8,128)(2,1)S(1)} %copy-done.22), channel_id=1, source_target_pairs={{0,1},{1,0},{2,3},{3,2},{4,5},{5,4},{6,7},{7,6},{8,9},{9,8},{10,11... | collective-permute-start | bytes 1179656 | tf_op jit(solution)/shard_map/ppermute | solution.py:571
  345.0 23.7 %collective-permute-start.12 = (bf16[2,2,1,1,2,24,2432]{6,5,4,3,2,1,0:T(8,128)(2,1)S(1)}, bf16[2,2,1,1,2,24,2432]{6,5,4,3,2,1,0:T(8,128)(2,1)S(1)}, u32[]{:S(2)}, u32[]{:S(2)}) collective-permute-start(bf16[2,2,1,1,2,24,2432]{6,5,4,3,2,1,0:T(8,128)(2,1)S(1)} %constant_dynamic-slice_fusion.18), channel_id=1, source_target_pairs={{0,4},{2,6},{4,0},{6,2},{8,12},{10,14},{12,8},{14,10},{16,20},{18,... | collective-permute-start | bytes 2801672 | tf_op jit(solution)/shard_map/ppermute | solution.py:524
  350.4 43.5 %collective-permute-start.27 = (bf16[2,2,1,1,2,96,768]{6,5,4,3,2,1,0:T(8,128)(2,1)S(1)}, bf16[2,2,1,1,2,96,768]{6,5,4,3,2,1,0:T(8,128)(2,1)S(1)}, u32[]{:S(2)}, u32[]{:S(2)}) collective-permute-start(bf16[2,2,1,1,2,96,768]{6,5,4,3,2,1,0:T(8,128)(2,1)S(1)} %constant_dynamic-slice_fusion.3), channel_id=1, source_target_pairs={{0,4},{2,6},{4,0},{6,2},{8,12},{10,14},{12,8},{14,10},{16,20},{18,... | collective-permute-start | bytes 3538952 | tf_op jit(solution)/shard_map/ppermute | solution.py:524
  369.0 9.9 %collective-permute-start.13 = (bf16[2,1,1,1,2,24,2432]{6,5,4,3,2,1,0:T(8,128)(2,1)S(1)}, bf16[2,1,1,1,2,24,2432]{6,5,4,3,2,1,0:T(8,128)(2,1)S(1)}, u32[]{:S(2)}, u32[]{:S(2)}) collective-permute-start(bf16[2,1,1,1,2,24,2432]{6,5,4,3,2,1,0:T(8,128)(2,1)S(1)} %constant_dynamic-slice_fusion.17), channel_id=1, source_target_pairs={{0,8},{2,10},{4,12},{6,14},{8,0},{10,2},{12,4},{14,6},{16,24},{18,... | collective-permute-start | bytes 1400840 | tf_op jit(solution)/shard_map/ppermute | solution.py:524
  381.9 31.8 %collective-permute-start.22 = (bf16[2,2,1,1,2,24,3072]{6,5,4,3,2,1,0:T(8,128)(2,1)S(1)}, bf16[2,2,1,1,2,24,3072]{6,5,4,3,2,1,0:T(8,128)(2,1)S(1)}, u32[]{:S(2)}, u32[]{:S(2)}) collective-permute-start(bf16[2,2,1,1,2,24,3072]{6,5,4,3,2,1,0:T(8,128)(2,1)S(1)} %constant_dynamic-slice_fusion.8), channel_id=1, source_target_pairs={{0,4},{2,6},{4,0},{6,2},{8,12},{10,14},{12,8},{14,10},{16,20},{18,... | collective-permute-start | bytes 3538952 | tf_op jit(solution)/shard_map/ppermute | solution.py:524
  388.8 28.1 %collective-permute-start.15 = (bf16[1,1,1,1,1,24,2432]{6,5,4,3,2,1,0:T(8,128)(2,1)S(1)}, bf16[1,1,1,1,1,24,2432]{6,5,4,3,2,1,0:T(8,128)(2,1)S(1)}, u32[]{:S(2)}, u32[]{:S(2)}) collective-permute-start(bf16[1,1,1,1,1,24,2432]{6,5,4,3,2,1,0:T(8,128)(2,1)S(1)} %constant_dynamic-slice_fusion.15), channel_id=1, source_target_pairs={{0,1},{1,0},{2,3},{3,2},{4,5},{5,4},{6,7},{7,6},{8,9},{9,8},{10,11... | collective-permute-start | bytes 350216 | tf_op jit(solution)/shard_map/ppermute | solution.py:524
  394.3 26.0 %collective-permute-start.28 = (bf16[2,1,1,1,2,96,768]{6,5,4,3,2,1,0:T(8,128)(2,1)S(1)}, bf16[2,1,1,1,2,96,768]{6,5,4,3,2,1,0:T(8,128)(2,1)}, u32[]{:S(2)}, u32[]{:S(2)}) collective-permute-start(bf16[2,1,1,1,2,96,768]{6,5,4,3,2,1,0:T(8,128)(2,1)S(1)} %constant_dynamic-slice_fusion.2), channel_id=1, source_target_pairs={{0,8},{2,10},{4,12},{6,14},{8,0},{10,2},{12,4},{14,6},{16,24},{18,... | collective-permute-start | bytes 1769480 | tf_op jit(solution)/shard_map/ppermute | solution.py:524
  415.0 16.6 %collective-permute-start.23 = (bf16[2,1,1,1,2,24,3072]{6,5,4,3,2,1,0:T(8,128)(2,1)}, bf16[2,1,1,1,2,24,3072]{6,5,4,3,2,1,0:T(8,128)(2,1)}, u32[]{:S(2)}, u32[]{:S(2)}) collective-permute-start(bf16[2,1,1,1,2,24,3072]{6,5,4,3,2,1,0:T(8,128)(2,1)} %constant_dynamic-slice_fusion.7), channel_id=1, source_target_pairs={{0,8},{2,10},{4,12},{6,14},{8,0},{10,2},{12,4},{14,6},{16,24},{18,... | collective-permute-start | bytes 1769480 | tf_op jit(solution)/shard_map/ppermute | solution.py:524
  421.5 21.3 %collective-permute-start.29 = (bf16[1,1,1,1,2,96,768]{6,5,4,3,2,1,0:T(8,128)(2,1)S(1)}, bf16[1,1,1,1,2,96,768]{6,5,4,3,2,1,0:T(8,128)(2,1)S(1)}, u32[]{:S(2)}, u32[]{:S(2)}) collective-permute-start(bf16[1,1,1,1,2,96,768]{6,5,4,3,2,1,0:T(8,128)(2,1)S(1)} %constant_dynamic-slice_fusion.1), channel_id=1, source_target_pairs={{0,16},{2,18},{4,20},{6,22},{8,24},{10,26},{12,28},{14,30},{16,0},... | collective-permute-start | bytes 884744 | tf_op jit(solution)/shard_map/ppermute | solution.py:524
  432.9 13.1 %collective-permute-start.24 = (bf16[1,1,1,1,2,24,3072]{6,5,4,3,2,1,0:T(8,128)(2,1)S(1)}, bf16[1,1,1,1,2,24,3072]{6,5,4,3,2,1,0:T(8,128)(2,1)S(1)}, u32[]{:S(2)}, u32[]{:S(2)}) collective-permute-start(bf16[1,1,1,1,2,24,3072]{6,5,4,3,2,1,0:T(8,128)(2,1)S(1)} %constant_dynamic-slice_fusion.6), channel_id=1, source_target_pairs={{0,16},{2,18},{4,20},{6,22},{8,24},{10,26},{12,28},{14,30},{16,0},... | collective-permute-start | bytes 884744 | tf_op jit(solution)/shard_map/ppermute | solution.py:524
  (37 other events, 657.8 us)
